TPU v7x, 32 devices: a whole 2x2x4 slice. The times are simulated.
32 devices in a mesh: groups: 2 (over y), seq: 4 (over z), mp: 2 (over x), section: 2 (over core).
Axes of the slice: x: 2, y: 2, z: 4, core: 2. Of those that a mesh axis runs over, the one named last changes fastest.
Arguments:
- readout: bfloat16 [8, 64, 32, 1024], P(('groups', 'mp', 'section'), None, 'seq'), parts along dimension 0, may hold values from -6 to 6
- first_kernel: bfloat16 [3, 3, 64, 128], replicated, may hold values from -0.25 to 0.25
- second_kernel: bfloat16 [3, 3, 128, 256], replicated, may hold values from -0.1875 to 0.1875
- embed_weight: bfloat16 [1024, 768], P(('mp', 'section')), may hold values from -0.1875 to 0.1875
- project_weight: bfloat16 [768, 2304], P(('mp', 'section'))
- output_weight: bfloat16 [768, 768], P(('mp', 'section')), may hold values from -0.4375 to 0.4375
- order: int32 [8, 512], P(('groups', 'mp', 'section')), parts along dimension 0, may hold values from 0 to 511, as said below
- active: int32 [8, 512], P(('groups', 'mp', 'section'), 'seq'), parts along dimension 0, may hold values 0 or 1
Outputs:
- encoded: bfloat16 [8, 512, 768], P(('groups', 'mp', 'section'), 'seq'), parts along dimension 0
There are 2 independent parts, one for each index of `groups`. A program takes and returns all parts, laid end to end along the dimension named above; an argument that names none is the same for every part. Nothing has to cross between parts.
Inputs may be any that keep to these rules, and one draw needn't show every extreme that they name: Each row of order lists each of the 512 patches of its region once. Patch i comes from the wire tile i // 128; each block of 128 positions k * 128 to (k + 1) * 128 - 1 holds exactly 32 patches of every wire tile.
All inputs are finite; a program needn't handle non-finite values. No bound on the sum of `active` on one device may be relied on, other than what follows from the above.
Results may differ from a plain program's by a relative error of at most 0.017.
Values may be sent and summed in bfloat16 or wider, within the bound.
No kernel may reach another device: no remote copies, remote signals or barrier semaphores. Data moves between devices by JAX's collectives and lax.ppermute only.
A program may use at most 64 MiB of HBM per device.

v0:
```python
import jax
import jax.numpy as jnp
from jax import lax
from jax.sharding import PartitionSpec as P

HEADS = 12


masked_score = -1e30
epsilon = 1e-05


def shifted(value, axis, steps):
    count = lax.axis_size(axis)
    first, last = (max(0, -steps), min(count, count - steps))
    return lax.ppermute(value, axis, [(source, source + steps) for source in range(first, last)])


def strided_conv(padded, kernel):
    result = lax.conv_general_dilated(
        padded[None],
        kernel,
        (2, 2),
        "VALID",
        dimension_numbers=("NCHW", "HWIO", "NCHW"),
        preferred_element_type=jnp.float32,
    )[0]
    return jax.nn.silu(result).astype(jnp.bfloat16)


def extend_low(tile, lower_row):
    joined = jnp.concatenate([lower_row, tile], axis=1)
    return jnp.pad(joined, ((0, 0), (0, 0), (1, 0)))


def normalize(tokens):
    values = tokens.astype(jnp.float32)
    center = jnp.mean(values, axis=-1, keepdims=True)
    spread = jnp.mean(jnp.square(values - center), axis=-1, keepdims=True)
    return ((values - center) * lax.rsqrt(spread + epsilon)).astype(jnp.bfloat16)


def patch_rows(features):
    channels, height, length = features.shape
    grid = features.reshape(channels, height // 2, 2, length // 2, 2)
    return grid.transpose(1, 3, 0, 2, 4).reshape(height // 2 * (length // 2), channels * 4)


def accumulate(carry, query_heads, query_pos, keys_piece, values_piece, flag_piece):
    summed, running, weight_sum = carry
    length = keys_piece.shape[0]
    head_count = query_heads.shape[1]
    head_size = query_heads.shape[2]
    key_heads = keys_piece.reshape(length, head_count, head_size)
    value_heads = values_piece.reshape(length, head_count, head_size)
    scores = jnp.einsum("qhd,khd->qhk", query_heads, key_heads, preferred_element_type=jnp.float32)
    key_pos = jnp.arange(length, dtype=jnp.int32)
    allowed = ((flag_piece[None, :] > 0.5) | (key_pos[None, :] == query_pos[:, None]))[:, None, :]
    scores = jnp.where(allowed, scores, masked_score)
    updated = jnp.maximum(running, jnp.max(scores, axis=-1))
    weights = jnp.where(allowed, jnp.exp(scores - updated[..., None]), 0.0)
    factor = jnp.exp(running - updated)
    added = jnp.einsum(
        "qhk,khd->qhd",
        weights.astype(jnp.bfloat16),
        value_heads,
        preferred_element_type=jnp.float32,
    )
    return (
        summed * factor[..., None] + added,
        updated,
        weight_sum * factor + jnp.sum(weights, axis=-1),
    )


def empty_state(rows, head_count, head_size):
    return (
        jnp.zeros((rows, head_count, head_size), jnp.float32),
        jnp.full((rows, head_count), masked_score, jnp.float32),
        jnp.zeros((rows, head_count), jnp.float32),
    )


def body(
    readout, first_kernel, second_kernel, embed_weight, project_weight, output_weight, order, active
):
    shards = lax.axis_size("seq")
    position = lax.axis_index("seq")
    embed_full, project_full, output_full = (
        lax.all_gather(embed_weight, ("mp", "section"), axis=0, tiled=True),
        lax.all_gather(project_weight, ("mp", "section"), axis=0, tiled=True),
        lax.all_gather(output_weight, ("mp", "section"), axis=0, tiled=True),
    )
    level_zero = readout[0]
    lower_first = shifted(level_zero[:, -1:, :], "seq", 1)
    level_one = strided_conv(extend_low(level_zero, lower_first), first_kernel)
    lower_second = shifted(level_one[:, -1:, :], "seq", 1)
    level_two = strided_conv(extend_low(level_one, lower_second), second_kernel)
    patches = patch_rows(level_two)
    count = patches.shape[0]
    group = count // shards
    width = embed_full.shape[1]
    sequence = order[0]
    blocks = sequence.reshape(shards, count)
    columns = jnp.arange(count, dtype=jnp.int32)
    ranked = jnp.where(blocks // count == position, count - columns[None, :], 0)
    picked = lax.top_k(ranked, group)[1]
    outgoing_rows = (jnp.take_along_axis(blocks, picked, axis=1) % count).reshape(-1)
    own_block = lax.dynamic_slice_in_dim(sequence, position * count, count)
    source = own_block // count
    member = (source[:, None] == jnp.arange(shards, dtype=jnp.int32)[None, :]).astype(jnp.int32)
    earlier = jnp.sum((jnp.cumsum(member, axis=0) - member) * member, axis=1)
    arrival = source * group + earlier
    outgoing = patches[outgoing_rows].reshape(shards, group, patches.shape[1])
    received = lax.all_to_all(outgoing, "seq", split_axis=0, concat_axis=0, tiled=True)
    placed = received.reshape(count, patches.shape[1])[arrival]
    tokens = jnp.dot(placed, embed_full, preferred_element_type=jnp.float32).astype(jnp.bfloat16)
    normed = normalize(tokens)
    head_size = width // HEADS
    projected = jnp.dot(normed, project_full, preferred_element_type=jnp.float32)
    query_flat = (projected[:, :width] * head_size ** (-0.5)).astype(jnp.bfloat16)
    queries = query_flat.reshape(count, HEADS, head_size)
    query_pos = position * count + columns
    flags = active[0].astype(jnp.bfloat16)
    initial = empty_state(count, HEADS, head_size)
    keys_flat = projected[:, width : 2 * width].astype(jnp.bfloat16)
    values_flat = projected[:, 2 * width :].astype(jnp.bfloat16)
    summed, running, weight_sum = accumulate(
        initial,
        queries,
        query_pos,
        lax.all_gather(keys_flat, "seq", axis=0, tiled=True),
        lax.all_gather(values_flat, "seq", axis=0, tiled=True),
        lax.all_gather(flags, "seq", axis=0, tiled=True),
    )
    mixed = (summed / weight_sum[..., None]).astype(jnp.bfloat16).reshape(count, width)
    result = tokens.astype(jnp.float32) + jnp.dot(
        mixed, output_full, preferred_element_type=jnp.float32
    )
    return result.astype(jnp.bfloat16)[None]


def solution(mesh):
    in_specs = (
        P(("groups", "mp", "section"), None, "seq", None),
        P(),
        P(),
        P(("mp", "section"), None),
        P(("mp", "section"), None),
        P(("mp", "section"), None),
        P(("groups", "mp", "section"), None),
        P(("groups", "mp", "section"), "seq"),
    )
    out_specs = P(("groups", "mp", "section"), "seq", None)
    return jax.shard_map(body, mesh=mesh, in_specs=in_specs, out_specs=out_specs, check_vma=False)
```

profile of v0, /device:TPU:0, one launch (start us, length us, event | category | flops | bytes accessed | tf_op | source)
XLA Modules:
  0.0 125.3 jit_solution(1145322353449359863)
XLA Ops:
  7.4 1.4 %fusion.63 = s32[4,128]{1,0:T(4,128)} fusion(s32[4,128]{1,0:T(4,128)} %bitcast.108, s32[128]{0:T(128)S(1)} %iota_subtract_fusion, s32[]{:T(128)S(6)} %axis_index.15), kind=kLoop, calls=%fused_computation.91 | loop fusion | flops 8704 | bytes 4612 | tf_op jit(solution)/shard_map/jit(_where)/select_n | solution.py:106
  10.6 1.5 %slice.34 = bf16[64,1,1024]{2,1,0:T(2,128)(2,1)S(1)} slice(bf16[64,8,1024]{2,1,0:T(8,128)(2,1)} %bitcast.116), slice={[0:64], [7:8], [0:1024]} | slice | bytes 262144 | tf_op jit(solution)/shard_map/slice | solution.py:95
  12.1 5.0 %collective-permute-start = (bf16[64,1,1024]{2,1,0:T(2,128)(2,1)S(1)}, bf16[64,1,1024]{2,1,0:T(2,128)(2,1)S(1)}, u32[]{:S(2)}, u32[]{:S(2)}) collective-permute-start(bf16[64,1,1024]{2,1,0:T(2,128)(2,1)S(1)} %slice.34), channel_id=1, source_target_pairs={{0,4},{4,8},{8,12},{1,5},{5,9},{9,13},{2,6},{6,10},{10,14},{3,7},{... | collective-permute-start | bytes 393224 | tf_op jit(solution)/shard_map/ppermute | solution.py:16
  19.1 1.5 %gather_fusion.2 = s32[128]{0:T(128)S(1)} fusion(s32[4,128]{1,0:T(4,128)S(1)} %bitcast.109, s32[128]{0:T(128)S(1)} %reshape.338), kind=kCustom, calls=%fused_computation.2 | custom fusion | bytes 2048 | tf_op jit(solution)/shard_map/jit(take_along_axis)/gather | solution.py:108
  21.5 1.2 collective-permute-done
  22.6 2.4 %fusion.14 = bf16[64,9,1,1025]{3,1,0,2:T(8,128)(2,1)S(1)} fusion(bf16[64,8,1024]{2,1,0:T(8,128)(2,1)S(1)} %bitcast.117, bf16[64,1,1024]{2,1,0:T(2,128)(2,1)S(1)} %collective-permute-done), kind=kLoop, calls=%fused_computation.20 | loop fusion | flops 4132800 | bytes 2360448 | tf_op jit(solution)/shard_map/broadcast_in_dim | solution.py:21
  25.3 4.4 %reshape.352 = bf16[64,9,1,8,130]{4,3,1,0,2:T(8,128)(2,1)} reshape(bf16[64,9,1,1040]{3,1,0,2:T(8,128)(2,1)S(1)} %pad.10) | data formatting | bytes 2396160 | tf_op jit(solution)/shard_map/conv_general_dilated | solution.py:20
  29.8 6.0 %copy.29 = bf16[64,9,1,8,130]{0,3,4,1,2:T(8,128)(2,1)S(1)} copy(bf16[64,9,1,8,130]{4,3,1,0,2:T(8,128)(2,1)} %reshape.352) | data formatting | bytes 2396160 | tf_op jit(solution)/shard_map/conv_general_dilated | solution.py:20
  35.8 1.1 fusion.24
  38.0 4.4 %collective-permute-start.1 = (bf16[128,1,512]{0,1,2:T(2,128)(2,1)S(1)}, bf16[128,1,512]{0,1,2:T(2,128)(2,1)S(1)}, u32[]{:S(2)}, u32[]{:S(2)}) collective-permute-start(bf16[128,1,512]{0,1,2:T(2,128)(2,1)S(1)} %slice.37), channel_id=1, source_target_pairs={{0,4},{4,8},{8,12},{1,5},{5,9},{9,13},{2,6},{6,10},{10,14},{3,7},{... | collective-permute-start | bytes 393224 | tf_op jit(solution)/shard_map/ppermute | solution.py:16
  42.4 4.6 %collective-permute-done.1 = bf16[128,1,512]{0,1,2:T(2,128)(2,1)S(1)} collective-permute-done((bf16[128,1,512]{0,1,2:T(2,128)(2,1)S(1)}, bf16[128,1,512]{0,1,2:T(2,128)(2,1)S(1)}, u32[]{:S(2)}, u32[]{:S(2)}) %collective-permute-start.1) | collective-permute-done | bytes 131104 | tf_op jit(solution)/shard_map/ppermute | solution.py:16
  50.2 1.6 %gather_fusion = bf16[128,1024]{1,0:T(8,128)(2,1)} fusion(bf16[128,1024]{1,0:T(8,128)(2,1)S(1)} %copy.38, s32[1024]{0:T(1024)S(1)} %pad_clamp_fusion.1), kind=kCustom, calls=%fused_computation | custom fusion | bytes 524800 | tf_op jit(solution)/shard_map/gather | solution.py:114
  51.8 5.8 %all-to-all-start = ((bf16[4,32,1024]{2,1,0:T(8,128)(2,1)}), bf16[4,32,1024]{2,1,0:T(8,128)(2,1)S(1)}, u32[]{:S(2)}, u32[]{:S(2)}) async-start(bf16[4,32,1024]{2,1,0:T(8,128)(2,1)} %bitcast.19), calls=%async_computation | async-start | bytes 524288 | tf_op jit(solution)/shard_map/all_to_all | solution.py:115
  57.5 11.6 %all-gather = bf16[1,512]{1,0:T(2,128)(2,1)S(1)} all-gather(bf16[1,128]{1,0:T(2,128)(2,1)S(1)} %convert_element_type.55), channel_id=2, replica_groups=mesh['groups'=2,'seq'=4,'mp'=2,'section'=2] {'seq'}, dimensions={1}, use_global_device_ids=true | all-gather | bytes 1280 | tf_op jit(solution)/shard_map/all_gather | solution.py:134
  69.1 0.8 fusion.55
  69.9 0.9 gather_fusion.1
  70.8 1.9 %fusion.77 = (f32[128]{0:T(128)S(1)}, f32[128,768]{1,0:T(8,128)S(1)}) fusion(bf16[128,1024]{1,0:T(8,128)(2,1)S(1)} %gather_fusion.1, bf16[1024,768]{1,0:T(8,128)(2,1)} %all-gather.5.cloned.1.call-done), kind=kOutput, calls=%fused_computation.119 | convolution fusion | flops 201621376 | bytes 2228736 | tf_op jit(solution)/shard_map/dot_general | solution.py:117
  72.9 3.9 %fusion.78 = (bf16[128,2304]{1,0:T(8,128)(2,1)S(1)}, f32[128,2304]{1,0:T(8,128)}) fusion(bf16[768,2304]{1,0:T(8,128)(2,1)} %all-gather.7.cloned.1.call-done, f32[128,768]{1,0:T(8,128)S(1)} %get-tuple-element.14, f32[128]{0:T(128)S(1)} %add_rsqrt_fusion, f32[128]{0:T(128)S(1)} %broadcast_multiply_fusion), kind=kOutput, calls=%fused_computation.120 | convolution fusion | flops 453574656 | bytes 5702656 | tf_op jit(solution)/shard_map/dot_general | solution.py:120
  76.8 16.6 %all_gather.21 = bf16[512,768]{1,0:T(8,128)(2,1)S(1)} all-gather(bf16[128,768]{1,0:T(8,128)(2,1)S(1)} %get-tuple-element.9), channel_id=1, replica_groups=mesh['groups'=2,'seq'=4,'mp'=2,'section'=2] {'seq'}, dimensions={0}, use_global_device_ids=true | all-gather | bytes 983040 | tf_op jit(solution)/shard_map/all_gather | solution.py:132
  93.7 1.0 fusion.52
  94.9 16.9 %all_gather.22 = bf16[512,768]{1,0:T(8,128)(2,1)S(1)} all-gather(bf16[128,768]{1,0:T(8,128)(2,1)S(1)} %get-tuple-element.10), channel_id=1, replica_groups=mesh['groups'=2,'seq'=4,'mp'=2,'section'=2] {'seq'}, dimensions={0}, use_global_device_ids=true | all-gather | bytes 983040 | tf_op jit(solution)/shard_map/all_gather | solution.py:133
  112.1 1.6 %fusion.3 = (f32[128,12]{0,1:T(8,128)S(1)}, f32[12,512,128]{2,1,0:T(8,128)S(1)}) fusion(pred[128,512]{0,1:T(8,128)(4,1)} %fusion.55, bf16[512,12,64]{0,2,1:T(8,128)(2,1)S(1)} %bitcast.113, bf16[128,12,64]{0,2,1:T(8,128)(2,1)S(1)} %bitcast.119), kind=kOutput, calls=%fused_computation.10 | convolution fusion | flops 102234624 | bytes 4200448 | tf_op jit(solution)/shard_map/qhd,khd->qhk/dot_general | solution.py:56
  114.4 1.0 fusion.43
  115.4 2.3 %fusion.36 = bf16[1,128,768]{2,1,0:T(8,128)(2,1)} fusion(f32[128,768]{1,0:T(8,128)S(1)} %get-tuple-element.14, bf16[128,768]{0,1:T(8,128)(2,1)S(1)} %bitcast.121, bf16[768,768]{1,0:T(8,128)(2,1)} %all-gather.9.cloned.1.call-done), kind=kOutput, calls=%fused_computation.40 | convolution fusion | flops 151191552 | bytes 1966080 | tf_op jit(solution)/shard_map/dot_general | solution.py:137
  (73 shorter events, 10.7 us)
Async XLA Ops:
  7.4 40.7 %copy-start = (bf16[3,3,128,256]{3,2,1,0:T(8,128)(2,1)S(1)}, bf16[3,3,128,256]{3,2,1,0:T(8,128)(2,1)}, u32[]{:S(2)}) copy-start(bf16[3,3,128,256]{3,2,1,0:T(8,128)(2,1)} %param.10) | copy-start | bytes 1769476
  7.4 10.9 %copy-start.1 = (s32[1,512]{1,0:T(1,128)S(1)}, s32[1,512]{1,0:T(1,128)}, u32[]{:S(2)}) copy-start(s32[1,512]{1,0:T(1,128)} %param.14) | copy-start | bytes 6148
  7.4 15.3 %copy-start.2 = (bf16[1,64,8,1024]{3,2,1,0:T(8,128)(2,1)S(1)}, bf16[1,64,8,1024]{3,2,1,0:T(8,128)(2,1)}, u32[]{:S(2)}) copy-start(bf16[1,64,8,1024]{3,2,1,0:T(8,128)(2,1)} %param.8) | copy-start | bytes 3145732
  7.4 10.9 %top_k.24.cloned.1.call-start = ((), (), s32[]{:S(2)}) async-start(), calls=%async_computation.4 | async-start | bytes 12320 | tf_op jit(solution)/shard_map/top_k | solution.py:107
  9.4 61.4 %all-gather.5.cloned.1.call-start = ((), (), s32[]{:S(2)}) async-start(), calls=%async_computation.1 | async-start | bytes 1966080 | tf_op jit(solution)/shard_map/all_gather | solution.py:90
  10.0 62.9 %all-gather.7.cloned.1.call-start = ((), (), s32[]{:S(2)}) async-start(), calls=%async_computation.2 | async-start | bytes 4423680 | tf_op jit(solution)/shard_map/all_gather | solution.py:91
  10.6 104.8 %all-gather.9.cloned.1.call-start = ((), (), s32[]{:S(2)}) async-start(), calls=%async_computation.3 | async-start | bytes 1474560 | tf_op jit(solution)/shard_map/all_gather | solution.py:92
  12.1 10.5 %collective-permute-start = (bf16[64,1,1024]{2,1,0:T(2,128)(2,1)S(1)}, bf16[64,1,1024]{2,1,0:T(2,128)(2,1)S(1)}, u32[]{:S(2)}, u32[]{:S(2)}) collective-permute-start(bf16[64,1,1024]{2,1,0:T(2,128)(2,1)S(1)} %slice.34), channel_id=1, source_target_pairs={{0,4},{4,8},{8,12},{1,5},{5,9},{9,13},{2,6},{6,10},{10,14},{3,7},{... | collective-permute-start | bytes 393224 | tf_op jit(solution)/shard_map/ppermute | solution.py:16
  29.8 6.0 %copy-start.4 = (bf16[3,3,64,128]{3,2,1,0:T(8,128)(2,1)S(1)}, bf16[3,3,64,128]{3,2,1,0:T(8,128)(2,1)}, u32[]{:S(2)}) copy-start(bf16[3,3,64,128]{3,2,1,0:T(8,128)(2,1)} %param.9) | copy-start | bytes 442372
  29.8 6.1 %copy-start.6 = (pred[8,65]{0,1:T(8,128)(4,1)S(1)}, pred[8,65]{0,1:T(8,128)(4,1)}, u32[]{:S(2)}) copy-start(pred[8,65]{0,1:T(8,128)(4,1)} %constant.110) | copy-start | bytes 1564
  38.0 9.1 %collective-permute-start.1 = (bf16[128,1,512]{0,1,2:T(2,128)(2,1)S(1)}, bf16[128,1,512]{0,1,2:T(2,128)(2,1)S(1)}, u32[]{:S(2)}, u32[]{:S(2)}) collective-permute-start(bf16[128,1,512]{0,1,2:T(2,128)(2,1)S(1)} %slice.37), channel_id=1, source_target_pairs={{0,4},{4,8},{8,12},{1,5},{5,9},{9,13},{2,6},{6,10},{10,14},{3,7},{... | collective-permute-start | bytes 393224 | tf_op jit(solution)/shard_map/ppermute | solution.py:16
  47.6 0.7 copy-start.7
  49.6 7.9 %copy-start.5 = (s32[1,128]{1,0:T(1,128)S(1)}, s32[1,128]{1,0:T(1,128)}, u32[]{:S(2)}) copy-start(s32[1,128]{1,0:T(1,128)} %param.15) | copy-start | bytes 1540
  51.8 18.1 %all-to-all-start = ((bf16[4,32,1024]{2,1,0:T(8,128)(2,1)}), bf16[4,32,1024]{2,1,0:T(8,128)(2,1)S(1)}, u32[]{:S(2)}, u32[]{:S(2)}) async-start(bf16[4,32,1024]{2,1,0:T(8,128)(2,1)} %bitcast.19), calls=%async_computation | async-start | bytes 524288 | tf_op jit(solution)/shard_map/all_to_all | solution.py:115
  112.1 1.6 %copy-start.3 = (pred[128,512]{0,1:T(8,128)(4,1)S(1)}, pred[128,512]{0,1:T(8,128)(4,1)}, u32[]{:S(2)}) copy-start(pred[128,512]{0,1:T(8,128)(4,1)} %fusion.55) | copy-start | bytes 196612
Sparse Core Ops, SparseCore 0:
  10.4 2.2 top_k.26.cloned.1.call-done
  (1 shorter events, 0.0 us)
Sparse Core Ops, SparseCore 1:
  11.4 22.2 all-gather.4
  35.1 30.6 all-gather.6
  67.2 17.3 all-gather.8
where the time goes:
time: 126 us; the launch traced here: 125 us
  blocking collectives  45.1 us (36%)
  local copies, waits for them, and re-layouts  20.1 us (16%)
  between operations  15.4 us (12%)
  starting transfers between devices  15.3 us (12%)
  matrix products  12.2 us (10%)
  other arithmetic  10.3 us (8%)
  waiting for transfers between devices  6.96 us (6%)
    all_gather x1, blocking collectives, body(): lax.all_gather(values_flat, 'seq', axis=0, tiled=True)  16.9 us
    all_gather x1, blocking collectives, body(): lax.all_gather(keys_flat, 'seq', axis=0, tiled=True)  16.6 us
    all_gather x1, blocking collectives, body(): lax.all_gather(flags, 'seq', axis=0, tiled=True)  11.6 us
    conv_general_dilated x8, local copies, waits for them, and re-layouts, strided_conv(): lax.conv_general_dilated(padded[None], kernel, (2, 2), 'VALID', dimension...  11.4 us
    ppermute x2, starting transfers between devices, shifted(): lax.ppermute(value, axis, [(source, source + steps) for source in range(f...  9.37 us
    ppermute x2, waiting for transfers between devices, shifted(): lax.ppermute(value, axis, [(source, source + steps) for source in range(f...  5.81 us
    all_to_all x1, starting transfers between devices, body(): lax.all_to_all(outgoing, 'seq', split_axis=0, concat_axis=0, tiled=True)  5.78 us
    dot_general x1, matrix products, body(): jnp.dot(normed, project_full, preferred_element_type=jnp.float32)  3.86 us
  transfers between devices with their start and end apart: 6, of which 2 were waited for; matrix products, arithmetic and copies ran while one was open for 30% of the time, Pallas kernels for 0%

commit v1 on v0

v1 whole, which is shorter than its diff:
```python
import functools

import jax
import jax.numpy as jnp
from jax import lax
from jax.experimental import pallas as pl
from jax.experimental.pallas import tpu as pltpu
from jax.sharding import PartitionSpec as P

HEADS = 12
masked_score = -1e30
epsilon = 1e-05
BF = jnp.bfloat16
F32 = jnp.float32
EXTRA = 8


def dot(a, b, ca=1, cb=0):
    return lax.dot_general(a, b, (((ca,), (cb,)), ((), ())), preferred_element_type=F32)


def iota(shape, axis):
    return lax.broadcasted_iota(jnp.int32, shape, axis)


def one_hot(mask):
    return jnp.where(mask, 1.0, 0.0).astype(BF)


def silu(v):
    half = 0.5 * v
    return half + half * jnp.tanh(half)


def split_matrix():
    row, col = iota((256, 256), 0), iota((256, 256), 1)
    return one_hot(row == jnp.where(col < 128, 2 * col, 2 * col - 255))


def split_time(rows, splitter):
    even, odd = [], []
    for start in range(0, rows.shape[1], 256):
        both = dot(rows[:, start : start + 256], splitter)
        even.append(both[:, :128])
        odd.append(both[:, 128:])
    if len(even) == 1:
        return even[0], odd[0]
    return jnp.concatenate(even, axis=1), jnp.concatenate(odd, axis=1)


def later(odd):
    moved = pltpu.roll(odd, 1, 1)
    return jnp.where(iota(odd.shape, 1) == 0, 0.0, moved)


def store_taps(taps, base, even, odd):
    height = even.shape[0]
    taps[base : base + height, :] = later(odd).astype(BF)
    taps[base + height : base + 2 * height, :] = even.astype(BF)
    taps[base + 2 * height : base + 3 * height, :] = odd.astype(BF)


def front_kernel(x_ref, k1_ref, msg_ref, taps1_ref, taps2_ref, all1, *, wires, channels, middle):
    splitter = split_matrix()
    row, col = iota((256, 256), 0), iota((256, 256), 1)
    part = 256 // wires
    mixer = one_hot(col == (row % part) * wires + row // part)
    for block in range(channels // part):
        rows = dot(mixer, x_ref[block * 256 : (block + 1) * 256, :]).astype(BF)
        even, odd = split_time(rows, splitter)
        lagged = later(odd)
        for wire in range(wires):
            here = slice(wire * part, (wire + 1) * part)
            base = wire * 3 * channels + block * part
            all1[base : base + part, :] = lagged[here].astype(BF)
            all1[base + channels : base + channels + part, :] = even[here].astype(BF)
            all1[base + 2 * channels : base + 2 * channels + part, :] = odd[here].astype(BF)
    taps1_ref[...] = all1[: 6 * channels, :]
    last = (wires - 1) * 3 * channels
    msg_ref[: 2 * channels, :] = all1[last + channels : last + 3 * channels, :]
    k1 = k1_ref[...]
    for level in range(1, wires // 2):
        start = (2 * level - 1) * 3 * channels
        out = silu(dot(k1, all1[start : start + 9 * channels, :], 0, 0)).astype(BF)
        if level == wires // 2 - 1:
            msg_ref[2 * channels :, :] = out
        even, odd = split_time(out, splitter)
        store_taps(taps2_ref, (level - 1) * 3 * middle, even, odd)


def back_kernel(
    block_ref, got_ref, taps1_ref, taps2_ref, k1_ref, k2_ref, active_ref, *refs, channels, middle, pieces
):
    embed_refs = refs[:pieces]
    out_ref, all1, all2, patch = refs[pieces:]
    splitter = split_matrix()
    length = got_ref.shape[1]
    odd = got_ref[channels : 2 * channels, :].astype(F32)
    all1[:channels, :] = later(odd).astype(BF)
    all1[channels : 3 * channels, :] = got_ref[: 2 * channels, :]
    all1[3 * channels :, :] = taps1_ref[...]
    first = silu(dot(k1_ref[...], all1[...], 0, 0)).astype(BF)
    even, odd = split_time(got_ref[2 * channels :, :], splitter)
    store_taps(all2, 0, even, odd)
    even, odd = split_time(first, splitter)
    store_taps(all2, 3 * middle, even, odd)
    rest = taps2_ref.shape[0]
    all2[6 * middle : 6 * middle + rest, :] = taps2_ref[...]
    k2 = k2_ref[...]
    outer = k2.shape[1]
    halves = []
    for level in range(2):
        start = level * 6 * middle
        out = silu(dot(k2, all2[start : start + 9 * middle, :], 0, 0)).astype(BF)
        even, odd = split_time(out, splitter)
        halves += [even.astype(BF), odd.astype(BF)]
    row, col = iota((256, 256), 0), iota((256, 256), 1)
    mixer = one_hot(col == (row % 4) * 64 + row // 4)
    for block in range(outer // 64):
        rows = jnp.concatenate([h[block * 64 : (block + 1) * 64] for h in halves], axis=0)
        patch[block * 256 : (block + 1) * 256, :] = dot(mixer, rows).astype(BF)
    total = None
    for piece, ref in enumerate(embed_refs):
        depth = ref.shape[0]
        base = pl.multiple_of(block_ref[piece] * depth, depth)
        term = dot(patch[pl.ds(base, depth), :], ref[...], 0, 0)
        total = term if total is None else total + term
    count, width = total.shape
    out_ref[:count, :] = total.astype(BF)
    tail = jnp.broadcast_to(active_ref[...].astype(F32), (EXTRA, count))
    tail = jnp.concatenate([tail, jnp.zeros((EXTRA, width - count), F32)], axis=1)
    out_ref[count:, :] = tail.astype(BF)


def attend_kernel(block_ref, got_ref, order_ref, *refs, pieces, shards, count):
    project_refs = refs[:pieces]
    output_refs = refs[pieces : 2 * pieces]
    out_ref, project, output, normed, tokens, keys, values, mixed, keep, sems = refs[2 * pieces :]
    copies = []
    for kind, (pieces_refs, target) in enumerate(((project_refs, project), (output_refs, output))):
        for piece, ref in enumerate(pieces_refs):
            depth = ref.shape[0]
            base = pl.multiple_of(block_ref[piece] * depth, depth)
            copy = pltpu.make_async_copy(ref, target.at[pl.ds(base, depth), :], sems.at[kind, piece])
            copy.start()
            copies.append(copy)
    width = got_ref.shape[1]
    size = shards * count
    stride = count + EXTRA
    for shard in range(shards):
        piece = got_ref[shard * stride : shard * stride + count, :]
        here = slice(shard * count, (shard + 1) * count)
        tokens[here, :] = piece
        value = piece.astype(F32)
        center = jnp.mean(value, axis=-1, keepdims=True)
        value = value - center
        spread = jnp.mean(value * value, axis=-1, keepdims=True)
        normed[here, :] = (value * lax.rsqrt(spread + epsilon)).astype(BF)
    square = iota((count, count), 0) == iota((count, count), 1)
    labels = iota((count, size), 1).astype(F32)

    def placed(row):
        across = jnp.broadcast_to(row.astype(F32), (count, count))
        down = jnp.sum(jnp.where(square, across, 0.0), axis=1, keepdims=True)
        return labels == down

    on = jnp.zeros((EXTRA, size), F32)
    for shard in range(shards):
        flags = got_ref[shard * stride + count : (shard + 1) * stride, :count]
        on += dot(flags, one_hot(placed(order_ref[shard : shard + 1, :])))
    position = block_ref[pieces]
    own = placed(order_ref[pl.ds(position, 1), :])
    select = one_hot(own)
    keep[...] = jnp.where(own | jnp.broadcast_to(on[:1] > 0.5, (count, size)), 1.0, 0.0)
    token_own = dot(select, tokens[...])
    normed_own = dot(select, normed[...]).astype(BF)
    for copy in copies[:pieces]:
        copy.wait()
    head = width // HEADS
    queries = (dot(normed_own, project[:, :width]) * head ** (-0.5)).astype(BF)
    keys[...] = dot(normed[...], project[:, width : 2 * width]).astype(BF)
    values[...] = dot(normed[...], project[:, 2 * width :]).astype(BF)
    for index in range(HEADS):
        here = slice(index * head, (index + 1) * head)
        scores = dot(queries[:, here], keys[:, here], 1, 1)
        allowed = keep[...] > 0.5
        scores = jnp.where(allowed, scores, masked_score)
        top = jnp.max(scores, axis=-1, keepdims=True)
        weights = jnp.exp(scores - top)
        total = jnp.sum(weights, axis=-1, keepdims=True)
        part = dot(weights.astype(BF), values[:, here]) / total
        mixed[:, here] = part.astype(BF)
    for copy in copies[pieces:]:
        copy.wait()
    out_ref[...] = (token_own + dot(mixed[...], output[...])).astype(BF)


def vmem():
    return pl.BlockSpec(memory_space=pltpu.VMEM)


def smem():
    return pl.BlockSpec(memory_space=pltpu.SMEM)


def hbm():
    return pl.BlockSpec(memory_space=pl.ANY)


def params():
    return pltpu.CompilerParams(vmem_limit_bytes=48 * 1024 * 1024)


def front(rows, k1, wires):
    channels = rows.shape[0] // wires
    middle = k1.shape[1]
    length = rows.shape[1] // 2
    return pl.pallas_call(
        functools.partial(front_kernel, wires=wires, channels=channels, middle=middle),
        out_shape=(
            jax.ShapeDtypeStruct((2 * channels + middle, length), BF),
            jax.ShapeDtypeStruct((6 * channels, length), BF),
            jax.ShapeDtypeStruct(((wires // 2 - 1) * 3 * middle, length // 2), BF),
        ),
        in_specs=[vmem()] * 2,
        out_specs=[vmem()] * 3,
        scratch_shapes=[pltpu.VMEM((wires * 3 * channels, length), BF)],
        compiler_params=params(),
        name="front",
    )(rows, k1)


def back(blocks, got, taps1, taps2, k1, k2, active, embeds):
    middle = k1.shape[1]
    channels = k1.shape[0] // 9
    length = got.shape[1]
    count = active.shape[1]
    width = embeds[0].shape[1]
    return pl.pallas_call(
        functools.partial(back_kernel, channels=channels, middle=middle, pieces=len(embeds)),
        out_shape=jax.ShapeDtypeStruct((count + EXTRA, width), BF),
        in_specs=[smem()] + [vmem()] * (6 + len(embeds)),
        out_specs=vmem(),
        scratch_shapes=[
            pltpu.VMEM((9 * channels, length), BF),
            pltpu.VMEM((15 * middle, length // 2), BF),
            pltpu.VMEM((4 * k2.shape[1], count), BF),
        ],
        compiler_params=params(),
        name="back",
    )(blocks, got, taps1, taps2, k1, k2, active, *embeds)


def attend(blocks, got, order, projects, outputs):
    shards, count = order.shape
    width = got.shape[1]
    size = shards * count
    pieces = len(projects)
    return pl.pallas_call(
        functools.partial(attend_kernel, pieces=pieces, shards=shards, count=count),
        out_shape=jax.ShapeDtypeStruct((count, width), BF),
        in_specs=[smem(), vmem(), vmem()] + [hbm()] * (2 * pieces),
        out_specs=vmem(),
        scratch_shapes=[
            pltpu.VMEM((width, 3 * width), BF),
            pltpu.VMEM((width, width), BF),
            pltpu.VMEM((size, width), BF),
            pltpu.VMEM((size, width), BF),
            pltpu.VMEM((size, width), BF),
            pltpu.VMEM((size, width), BF),
            pltpu.VMEM((count, width), BF),
            pltpu.VMEM((count, size), F32),
            pltpu.SemaphoreType.DMA((2, pieces)),
        ],
        compiler_params=params(),
        name="attend",
    )(blocks, got, order, *projects, *outputs)


def swapped(value, axis):
    return lax.ppermute(value, axis, [(0, 1), (1, 0)])


def gathered(weight):
    if lax.axis_size("mp") == 2 and lax.axis_size("section") == 2:
        across = swapped(weight, "mp")
        return [weight, swapped(weight, "section"), across, swapped(across, "section")]
    return [lax.all_gather(weight, ("mp", "section"), axis=0, tiled=True)]


def body(
    readout, first_kernel, second_kernel, embed_weight, project_weight, output_weight, order, active
):
    shards = lax.axis_size("seq")
    position = lax.axis_index("seq")
    embeds, projects, outputs = gathered(embed_weight), gathered(project_weight), gathered(output_weight)
    pieces = len(embeds)
    own = lax.axis_index("mp") * 2 + lax.axis_index("section") if pieces > 1 else 0
    blocks = jnp.concatenate(
        [jnp.arange(pieces, dtype=jnp.int32) ^ own, jnp.reshape(position, (1,)).astype(jnp.int32)]
    )
    channels, wires, ticks = readout.shape[1:]
    k1 = first_kernel.reshape(-1, first_kernel.shape[-1])
    k2 = second_kernel.reshape(-1, second_kernel.shape[-1])
    msg, taps1, taps2 = front(readout.reshape(channels * wires, ticks), k1, wires)
    got = lax.ppermute(msg, "seq", [(i, i + 1) for i in range(shards - 1)])
    tokens = back(blocks, got, taps1, taps2, k1, k2, active, embeds)
    everyone = lax.all_gather(tokens, "seq", axis=0, tiled=True)
    result = attend(blocks, everyone, order.reshape(shards, -1), projects, outputs)
    return result[None]


def solution(mesh):
    in_specs = (
        P(("groups", "mp", "section"), None, "seq", None),
        P(),
        P(),
        P(("mp", "section"), None),
        P(("mp", "section"), None),
        P(("mp", "section"), None),
        P(("groups", "mp", "section"), None),
        P(("groups", "mp", "section"), "seq"),
    )
    out_specs = P(("groups", "mp", "section"), "seq", None)
    return jax.shard_map(body, mesh=mesh, in_specs=in_specs, out_specs=out_specs, check_vma=False)
```

time: 126 us -> 87.4 us (0.69)
  waiting for transfers between devices: 6.96 us -> 33.6 us
  blocking collectives: 45.1 us -> 21.4 us
  between operations: 15.4 us -> 0.1 us
  Pallas kernels: 0 us -> 14.1 us
  matrix products: 12.2 us -> 0 us
  local copies, waits for them, and re-layouts: 20.1 us -> 8.09 us
  other arithmetic: 10.3 us -> 0.08 us
  starting transfers between devices: 15.3 us -> 9.59 us
    ppermute x2 -> x10, waiting for transfers between devices: 5.81 us -> 33.6 us  [the longest x9 28 us: swapped(): return lax.ppermute(value, axis, [(0, 1), (1, 0)])]
    all_gather x3 -> x1, blocking collectives: 45.1 us -> 21.4 us  [body(): everyone = lax.all_gather(tokens, 'seq', axis=0, tiled=True)]
    pallas_call x0 -> x3, Pallas kernels: none -> 14.1 us  [the longest x1 8.73 us: attend(): pl.pallas_call(functools.partial(attend_kernel, pieces=pieces, shards=sha...]
    conv_general_dilated x8 -> x0, local copies, waits for them, and re-layouts: 11.4 us -> none  [strided_conv(): lax.conv_general_dilated(padded[None], kernel, (2, 2), 'VALID', dimension...]
    dot_general x5 -> x0, matrix products: 10.6 us -> none  [the longest x1 3.86 us: body(): jnp.dot(normed, project_full, preferred_element_type=jnp.float32)]
    unnamed x17 -> x26, local copies, waits for them, and re-layouts: 0.29 us -> 8.09 us
    all_to_all x1 -> x0, starting transfers between devices: 5.78 us -> none  [body(): lax.all_to_all(outgoing, 'seq', split_axis=0, concat_axis=0, tiled=True)]
    gather x5 -> x0, local copies, waits for them, and re-layouts: 4.09 us -> none  [the longest x3 1.67 us: body(): jnp.take_along_axis(blocks, picked, axis=1) % count]
  transfers between devices with their start and end apart: 6 -> 10, of which waited for: 2 -> 3; matrix products, arithmetic and copies ran while one was open for 30% -> 0% of each run, Pallas kernels for 0% -> 6%
where the time goes in v1:
time: 87.4 us; the launch traced here: 87 us
  waiting for transfers between devices  33.6 us (38%)
  blocking collectives  21.4 us (24%)
  Pallas kernels  14.1 us (16%)
  starting transfers between devices  9.59 us (11%)
  local copies, waits for them, and re-layouts  8.09 us (9%)
    ppermute x9, waiting for transfers between devices, swapped(): return lax.ppermute(value, axis, [(0, 1), (1, 0)])  28 us
    all_gather x1, blocking collectives, body(): everyone = lax.all_gather(tokens, 'seq', axis=0, tiled=True)  21.4 us
    pallas_call x1, Pallas kernels, attend(): pl.pallas_call(functools.partial(attend_kernel, pieces=pieces, shards=sha...  8.73 us
    unnamed x26, local copies, waits for them, and re-layouts  8.09 us
    ppermute x1, waiting for transfers between devices, body(): got = lax.ppermute(msg, 'seq', [(i, i + 1) for i in range(shards - 1)])  5.63 us
    ppermute x9, starting transfers between devices, swapped(): return lax.ppermute(value, axis, [(0, 1), (1, 0)])  5.57 us
    ppermute x1, starting transfers between devices, body(): got = lax.ppermute(msg, 'seq', [(i, i + 1) for i in range(shards - 1)])  4.02 us
    pallas_call x1, Pallas kernels, back(): pl.pallas_call(functools.partial(back_kernel, channels=channels, middle=m...  3.64 us
  transfers between devices with their start and end apart: 10, of which 3 were waited for; matrix products, arithmetic and copies ran while one was open for 0% of the time, Pallas kernels for 6%

profile of v1, /device:TPU:0, one launch (start us, length us, event | category | flops | bytes accessed | tf_op | source)
XLA Modules:
  0.0 87.0 jit_solution(10315452731691963090)
XLA Ops:
  0.0 3.0 %collective-permute-start.5 = (bf16[192,2304]{1,0:T(8,128)(2,1)}, bf16[192,2304]{1,0:T(8,128)(2,1)S(1)}, u32[]{:S(2)}, u32[]{:S(2)}) collective-permute-start(bf16[192,2304]{1,0:T(8,128)(2,1)} %refs_0_.3), channel_id=1, source_target_pairs={{0,2},{2,0},{1,3},{3,1},{4,6},{6,4},{5,7},{7,5},{8,10},{10,8},{9,1... | collective-permute-start | bytes 2654216 | tf_op jit(solution)/shard_map/ppermute | solution.py:281
  3.0 0.0 collective-permute-start.2
  3.0 20.7 %collective-permute-done.5.refs_2_ = bf16[192,2304]{1,0:T(8,128)(2,1)S(1)} collective-permute-done((bf16[192,2304]{1,0:T(8,128)(2,1)}, bf16[192,2304]{1,0:T(8,128)(2,1)S(1)}, u32[]{:S(2)}, u32[]{:S(2)}) %collective-permute-start.5) | collective-permute-done | bytes 884768 | tf_op jit(solution)/shard_map/ppermute | solution.py:281
  23.7 1.2 %copy-done = bf16[1,64,8,1024]{3,2,1,0:T(8,128)(2,1)S(1)} copy-done((bf16[1,64,8,1024]{3,2,1,0:T(8,128)(2,1)S(1)}, bf16[1,64,8,1024]{3,2,1,0:T(8,128)(2,1)}, u32[]{:S(2)}) %copy-start) | copy-done | bytes 1048600
  24.9 0.9 %copy-done.2 = bf16[3,3,64,128]{3,2,1,0:T(8,128)(2,1)S(1)} copy-done((bf16[3,3,64,128]{3,2,1,0:T(8,128)(2,1)S(1)}, bf16[3,3,64,128]{3,2,1,0:T(8,128)(2,1)}, u32[]{:S(2)}) %copy-start.2) | copy-done | bytes 147480
  25.8 1.8 %front.1 = (bf16[256,512]{1,0:T(8,128)(2,1)S(1)}, bf16[384,512]{1,0:T(8,128)(2,1)S(1)}, bf16[1152,256]{1,0:T(8,128)(2,1)S(1)}) custom-call(bf16[512,1024]{1,0:T(8,128)(2,1)S(1)} %bitcast.6, bf16[576,128]{1,0:T(8,128)(2,1)S(1)} %bitcast.7), custom_call_target="tpu_custom_call" | custom-call | tf_op jit(solution)/shard_map/front/pallas_call | solution.py:218
  27.6 0.8 copy-done.5
  28.4 0.7 copy-done.7
  29.2 4.0 %collective-permute-start = (bf16[256,512]{1,0:T(8,128)(2,1)S(1)}, bf16[256,512]{1,0:T(8,128)(2,1)S(1)}, u32[]{:S(2)}, u32[]{:S(2)}) collective-permute-start(bf16[256,512]{1,0:T(8,128)(2,1)S(1)} %get-tuple-element.8), channel_id=1, source_target_pairs={{0,4},{4,8},{8,12},{1,5},{5,9},{9,13},{2,6},{6,10},{10,14},{3,7},{... | collective-permute-start | bytes 786440 | tf_op jit(solution)/shard_map/ppermute | solution.py:306
  33.2 0.3 collective-permute-start.1
  33.5 0.3 collective-permute-start.3
  33.8 5.6 %collective-permute-done.got_ref = bf16[256,512]{1,0:T(8,128)(2,1)S(1)} collective-permute-done((bf16[256,512]{1,0:T(8,128)(2,1)S(1)}, bf16[256,512]{1,0:T(8,128)(2,1)S(1)}, u32[]{:S(2)}, u32[]{:S(2)}) %collective-permute-start) | collective-permute-done | bytes 262176 | tf_op jit(solution)/shard_map/ppermute | solution.py:306
  39.4 0.7 copy-done.9
  40.1 1.5 %collective-permute-start.8 = (bf16[192,768]{1,0:T(8,128)(2,1)}, bf16[192,768]{1,0:T(8,128)(2,1)}, u32[]{:S(2)}, u32[]{:S(2)}) collective-permute-start(bf16[192,768]{1,0:T(8,128)(2,1)} %refs_4_.1), channel_id=1, source_target_pairs={{0,2},{2,0},{1,3},{3,1},{4,6},{6,4},{5,7},{7,5},{8,10},{10,8},{9,1... | collective-permute-start | bytes 884744 | tf_op jit(solution)/shard_map/ppermute | solution.py:281
  41.6 0.1 pad_add_fusion.block_ref
  41.7 7.3 %collective-permute-done.8.refs_6_ = bf16[192,768]{1,0:T(8,128)(2,1)} collective-permute-done((bf16[192,768]{1,0:T(8,128)(2,1)}, bf16[192,768]{1,0:T(8,128)(2,1)}, u32[]{:S(2)}, u32[]{:S(2)}) %collective-permute-start.8) | collective-permute-done | bytes 294944 | tf_op jit(solution)/shard_map/ppermute | solution.py:281
  49.0 0.5 collective-permute-start.9
  49.5 0.6 copy-done.12
  50.2 1.1 %copy-done.6 = bf16[1152,256]{1,0:T(8,128)(2,1)S(1)} copy-done((bf16[1152,256]{1,0:T(8,128)(2,1)S(1)}, bf16[1152,256]{1,0:T(8,128)(2,1)}, u32[]{:S(2)}) %copy-start.6) | copy-done | bytes 589848
  51.2 1.0 %copy-done.8 = bf16[384,512]{1,0:T(8,128)(2,1)S(1)} copy-done((bf16[384,512]{1,0:T(8,128)(2,1)S(1)}, bf16[384,512]{1,0:T(8,128)(2,1)}, u32[]{:S(2)}) %copy-start.8) | copy-done | bytes 393240
  52.2 0.9 %copy-done.10 = bf16[256,512]{1,0:T(8,128)(2,1)S(1)} copy-done((bf16[256,512]{1,0:T(8,128)(2,1)S(1)}, bf16[256,512]{1,0:T(8,128)(2,1)}, u32[]{:S(2)}) %copy-start.10) | copy-done | bytes 262168
  53.2 3.6 %back.1 = bf16[136,768]{1,0:T(8,128)(2,1)S(1)} custom-call(s32[5]{0:T(128)S(1)} %pad_add_fusion.block_ref, bf16[256,512]{1,0:T(8,128)(2,1)S(1)} %copy-done.10, bf16[384,512]{1,0:T(8,128)(2,1)S(1)} %copy-done.8, bf16[1152,256]{1,0:T(8,128)(2,1)S(1)} %copy-done.6, bf16[576,128]{1,0:T(8,128)(2,1)S(1)} %bitcast.8, bf16[1152,256]{1,0:T(8,128)(2,1)S(1)} %bitcast.9, ...), custom_call_target="tpu_custom_call" | custom-call | tf_op jit(solution)/shard_map/back/pallas_call | solution.py:239
  56.8 21.4 %all_gather.3.got_ref = bf16[544,768]{1,0:T(8,128)(2,1)S(1)} all-gather(bf16[136,768]{1,0:T(8,128)(2,1)S(1)} %back.1), channel_id=1, replica_groups=mesh['groups'=2,'seq'=4,'mp'=2,'section'=2] {'seq'}, dimensions={0}, use_global_device_ids=true | all-gather | bytes 1044480 | tf_op jit(solution)/shard_map/all_gather | solution.py:308
  78.3 8.7 %attend.1 = bf16[128,768]{1,0:T(8,128)(2,1)} custom-call(s32[5]{0:T(128)S(1)} %pad_add_fusion.block_ref, bf16[544,768]{1,0:T(8,128)(2,1)S(1)} %all_gather.3.got_ref, s32[4,128]{1,0:T(4,128)S(1)} %bitcast.10, bf16[192,2304]{1,0:T(8,128)(2,1)S(1)} %copy-done.1, bf16[192,2304]{1,0:T(8,128)(2,1)S(1)} %collective-permute-done.4.refs_1_, ...), custom_call_target="tpu_custom_call" | custom-call | tf_op jit(solution)/shard_map/attend/pallas_call | solution.py:259
  (28 shorter events, 0.1 us)
Async XLA Ops:
  0.0 23.7 %collective-permute-start.5 = (bf16[192,2304]{1,0:T(8,128)(2,1)}, bf16[192,2304]{1,0:T(8,128)(2,1)S(1)}, u32[]{:S(2)}, u32[]{:S(2)}) collective-permute-start(bf16[192,2304]{1,0:T(8,128)(2,1)} %refs_0_.3), channel_id=1, source_target_pairs={{0,2},{2,0},{1,3},{3,1},{4,6},{6,4},{5,7},{7,5},{8,10},{10,8},{9,1... | collective-permute-start | bytes 2654216 | tf_op jit(solution)/shard_map/ppermute | solution.py:281
  3.0 30.5 %collective-permute-start.2 = (bf16[256,768]{1,0:T(8,128)(2,1)}, bf16[256,768]{1,0:T(8,128)(2,1)}, u32[]{:S(2)}, u32[]{:S(2)}) collective-permute-start(bf16[256,768]{1,0:T(8,128)(2,1)} %refs_0_.2), channel_id=1, source_target_pairs={{0,2},{2,0},{1,3},{3,1},{4,6},{6,4},{5,7},{7,5},{8,10},{10,8},{9,1... | collective-permute-start | bytes 1179656 | tf_op jit(solution)/shard_map/ppermute | solution.py:281
  3.0 75.2 %collective-permute-start.4 = (bf16[192,2304]{1,0:T(8,128)(2,1)}, bf16[192,2304]{1,0:T(8,128)(2,1)S(1)}, u32[]{:S(2)}, u32[]{:S(2)}) collective-permute-start(bf16[192,2304]{1,0:T(8,128)(2,1)} %refs_0_.3), channel_id=1, source_target_pairs={{0,1},{1,0},{2,3},{3,2},{4,5},{5,4},{6,7},{7,6},{8,9},{9,8},{10,11... | collective-permute-start | bytes 2654216 | tf_op jit(solution)/shard_map/ppermute | solution.py:281
  23.7 54.6 %collective-permute-start.6 = (bf16[192,2304]{1,0:T(8,128)(2,1)S(1)}, bf16[192,2304]{1,0:T(8,128)(2,1)S(1)}, u32[]{:S(2)}, u32[]{:S(2)}) collective-permute-start(bf16[192,2304]{1,0:T(8,128)(2,1)S(1)} %collective-permute-done.5.refs_2_), channel_id=1, source_target_pairs={{0,1},{1,0},{2,3},{3,2},{4,5},{5,4},{6,7},{7,6},{8,9},{9,8},{10,11... | collective-permute-start | bytes 2654216 | tf_op jit(solution)/shard_map/ppermute | solution.py:281
  23.7 1.2 %copy-start = (bf16[1,64,8,1024]{3,2,1,0:T(8,128)(2,1)S(1)}, bf16[1,64,8,1024]{3,2,1,0:T(8,128)(2,1)}, u32[]{:S(2)}) copy-start(bf16[1,64,8,1024]{3,2,1,0:T(8,128)(2,1)} %param.8) | copy-start | bytes 3145732
  24.9 0.9 %copy-start.2 = (bf16[3,3,64,128]{3,2,1,0:T(8,128)(2,1)S(1)}, bf16[3,3,64,128]{3,2,1,0:T(8,128)(2,1)}, u32[]{:S(2)}) copy-start(bf16[3,3,64,128]{3,2,1,0:T(8,128)(2,1)} %param.9) | copy-start | bytes 442372
  25.8 23.7 %copy-start.3 = (bf16[3,3,64,128]{3,2,1,0:T(8,128)(2,1)S(1)}, bf16[3,3,64,128]{3,2,1,0:T(8,128)(2,1)}, u32[]{:S(2)}) copy-start(bf16[3,3,64,128]{3,2,1,0:T(8,128)(2,1)} %param.9) | copy-start | bytes 442372
  25.8 23.7 %copy-start.4 = (bf16[3,3,128,256]{3,2,1,0:T(8,128)(2,1)S(1)}, bf16[3,3,128,256]{3,2,1,0:T(8,128)(2,1)}, u32[]{:S(2)}) copy-start(bf16[3,3,128,256]{3,2,1,0:T(8,128)(2,1)} %param.10) | copy-start | bytes 1769476
  27.6 0.8 copy-start.5
  28.4 0.7 copy-start.7
  29.2 10.2 %collective-permute-start = (bf16[256,512]{1,0:T(8,128)(2,1)S(1)}, bf16[256,512]{1,0:T(8,128)(2,1)S(1)}, u32[]{:S(2)}, u32[]{:S(2)}) collective-permute-start(bf16[256,512]{1,0:T(8,128)(2,1)S(1)} %get-tuple-element.8), channel_id=1, source_target_pairs={{0,4},{4,8},{8,12},{1,5},{5,9},{9,13},{2,6},{6,10},{10,14},{3,7},{... | collective-permute-start | bytes 786440 | tf_op jit(solution)/shard_map/ppermute | solution.py:306
  33.2 15.8 %collective-permute-start.1 = (bf16[256,768]{1,0:T(8,128)(2,1)}, bf16[256,768]{1,0:T(8,128)(2,1)}, u32[]{:S(2)}, u32[]{:S(2)}) collective-permute-start(bf16[256,768]{1,0:T(8,128)(2,1)} %refs_0_.2), channel_id=1, source_target_pairs={{0,1},{1,0},{2,3},{3,2},{4,5},{5,4},{6,7},{7,6},{8,9},{9,8},{10,11... | collective-permute-start | bytes 1179656 | tf_op jit(solution)/shard_map/ppermute | solution.py:281
  33.5 16.0 %collective-permute-start.3 = (bf16[256,768]{1,0:T(8,128)(2,1)}, bf16[256,768]{1,0:T(8,128)(2,1)}, u32[]{:S(2)}, u32[]{:S(2)}) collective-permute-start(bf16[256,768]{1,0:T(8,128)(2,1)} %collective-permute-done.2.refs_2_), channel_id=1, source_target_pairs={{0,1},{1,0},{2,3},{3,2},{4,5},{5,4},{6,7},{7,6},{8,9},{9,8},{10,11... | collective-permute-start | bytes 1179656 | tf_op jit(solution)/shard_map/ppermute | solution.py:281
  39.4 0.7 copy-start.9
  40.1 8.9 %collective-permute-start.8 = (bf16[192,768]{1,0:T(8,128)(2,1)}, bf16[192,768]{1,0:T(8,128)(2,1)}, u32[]{:S(2)}, u32[]{:S(2)}) collective-permute-start(bf16[192,768]{1,0:T(8,128)(2,1)} %refs_4_.1), channel_id=1, source_target_pairs={{0,2},{2,0},{1,3},{3,1},{4,6},{6,4},{5,7},{7,5},{8,10},{10,8},{9,1... | collective-permute-start | bytes 884744 | tf_op jit(solution)/shard_map/ppermute | solution.py:281
  49.0 29.3 %collective-permute-start.7 = (bf16[192,768]{1,0:T(8,128)(2,1)}, bf16[192,768]{1,0:T(8,128)(2,1)S(1)}, u32[]{:S(2)}, u32[]{:S(2)}) collective-permute-start(bf16[192,768]{1,0:T(8,128)(2,1)} %refs_4_.1), channel_id=1, source_target_pairs={{0,1},{1,0},{2,3},{3,2},{4,5},{5,4},{6,7},{7,6},{8,9},{9,8},{10,11... | collective-permute-start | bytes 884744 | tf_op jit(solution)/shard_map/ppermute | solution.py:281
  49.0 29.2 %collective-permute-start.9 = (bf16[192,768]{1,0:T(8,128)(2,1)}, bf16[192,768]{1,0:T(8,128)(2,1)S(1)}, u32[]{:S(2)}, u32[]{:S(2)}) collective-permute-start(bf16[192,768]{1,0:T(8,128)(2,1)} %collective-permute-done.8.refs_6_), channel_id=1, source_target_pairs={{0,1},{1,0},{2,3},{3,2},{4,5},{5,4},{6,7},{7,6},{8,9},{9,8},{10,11... | collective-permute-start | bytes 884744 | tf_op jit(solution)/shard_map/ppermute | solution.py:281
  49.5 0.7 copy-start.12
  50.2 1.1 %copy-start.6 = (bf16[1152,256]{1,0:T(8,128)(2,1)S(1)}, bf16[1152,256]{1,0:T(8,128)(2,1)}, u32[]{:S(2)}) copy-start(bf16[1152,256]{1,0:T(8,128)(2,1)} %copy-done.5) | copy-start | bytes 1769476
  51.2 1.0 %copy-start.8 = (bf16[384,512]{1,0:T(8,128)(2,1)S(1)}, bf16[384,512]{1,0:T(8,128)(2,1)}, u32[]{:S(2)}) copy-start(bf16[384,512]{1,0:T(8,128)(2,1)} %copy-done.7) | copy-start | bytes 1179652
  52.2 0.9 %copy-start.10 = (bf16[256,512]{1,0:T(8,128)(2,1)S(1)}, bf16[256,512]{1,0:T(8,128)(2,1)}, u32[]{:S(2)}) copy-start(bf16[256,512]{1,0:T(8,128)(2,1)} %copy-done.9) | copy-start | bytes 786436
  56.8 21.4 %copy-start.1 = (bf16[192,2304]{1,0:T(8,128)(2,1)S(1)}, bf16[192,2304]{1,0:T(8,128)(2,1)}, u32[]{:S(2)}) copy-start(bf16[192,2304]{1,0:T(8,128)(2,1)} %refs_0_.3) | copy-start | bytes 2654212
  56.8 21.4 %copy-start.11 = (s32[1,512]{1,0:T(1,128)S(1)}, s32[1,512]{1,0:T(1,128)}, u32[]{:S(2)}) copy-start(s32[1,512]{1,0:T(1,128)} %param.14) | copy-start | bytes 6148

commit v2 on v1

v2 whole, which is shorter than its diff:
```python
import functools

import jax
import jax.numpy as jnp
from jax import lax
from jax.experimental import pallas as pl
from jax.experimental.pallas import tpu as pltpu
from jax.sharding import PartitionSpec as P


HEADS = 12
masked_score = -1e30
largest = 3e38
epsilon = 1e-05
BF = jnp.bfloat16
F32 = jnp.float32
EXTRA = 8


def dot(a, b, ca=1, cb=0):
    return lax.dot_general(a, b, (((ca,), (cb,)), ((), ())), preferred_element_type=F32)


def iota(shape, axis):
    return lax.broadcasted_iota(jnp.int32, shape, axis)


def one_hot(mask):
    return jnp.where(mask, 1.0, 0.0).astype(BF)


def silu(v):
    half = 0.5 * v
    return half + half * jnp.tanh(half)


def split_matrix():
    row, col = iota((256, 256), 0), iota((256, 256), 1)
    return one_hot(row == jnp.where(col < 128, 2 * col, 2 * col - 255))


def split_time(rows, splitter):
    even, odd = [], []
    for start in range(0, rows.shape[1], 256):
        both = dot(rows[:, start : start + 256], splitter)
        even.append(both[:, :128])
        odd.append(both[:, 128:])
    if len(even) == 1:
        return even[0], odd[0]
    return jnp.concatenate(even, axis=1), jnp.concatenate(odd, axis=1)


def later(odd):
    moved = pltpu.roll(odd, 1, 1)
    return jnp.where(iota(odd.shape, 1) == 0, 0.0, moved)


def store_taps(taps, base, even, odd):
    height = even.shape[0]
    taps[base : base + height, :] = later(odd).astype(BF)
    taps[base + height : base + 2 * height, :] = even.astype(BF)
    taps[base + 2 * height : base + 3 * height, :] = odd.astype(BF)


def front_kernel(x_ref, k1_ref, msg_ref, taps1_ref, taps2_ref, all1, *, wires, channels, middle):
    splitter = split_matrix()
    row, col = iota((256, 256), 0), iota((256, 256), 1)
    part = 256 // wires
    mixer = one_hot(col == (row % part) * wires + row // part)
    for block in range(channels // part):
        rows = dot(mixer, x_ref[block * 256 : (block + 1) * 256, :]).astype(BF)
        even, odd = split_time(rows, splitter)
        lagged = later(odd)
        for wire in range(wires):
            here = slice(wire * part, (wire + 1) * part)
            base = wire * 3 * channels + block * part
            all1[base : base + part, :] = lagged[here].astype(BF)
            all1[base + channels : base + channels + part, :] = even[here].astype(BF)
            all1[base + 2 * channels : base + 2 * channels + part, :] = odd[here].astype(BF)
    taps1_ref[...] = all1[: 6 * channels, :]
    last = (wires - 1) * 3 * channels
    msg_ref[: 2 * channels, :] = all1[last + channels : last + 3 * channels, :]
    k1 = k1_ref[...]
    for level in range(1, wires // 2):
        start = (2 * level - 1) * 3 * channels
        out = silu(dot(k1, all1[start : start + 9 * channels, :], 0, 0)).astype(BF)
        if level == wires // 2 - 1:
            msg_ref[2 * channels :, :] = out
        even, odd = split_time(out, splitter)
        store_taps(taps2_ref, (level - 1) * 3 * middle, even, odd)


def middle_kernel(
    block_ref, taps1_ref, taps2_ref, k1_ref, k2_ref, *refs, channels, middle, pieces
):
    embed_refs = refs[:pieces]
    first_ref, second_ref, token_ref, low_ref, high, patch = refs[pieces:]
    splitter = split_matrix()
    first_ref[...] = dot(k1_ref[3 * channels :, :], taps1_ref[...], 0, 0)
    second_ref[...] = dot(k2_ref[6 * middle :, :], taps2_ref[: 3 * middle, :], 0, 0)
    out = silu(dot(k2_ref[...], taps2_ref[...], 0, 0)).astype(BF)
    store_patch(patch, out, splitter)
    row, col = iota((256, 256), 0), iota((256, 256), 1)
    mixer = one_hot(col == (row % 64) * 4 + row // 64)
    for piece, ref in enumerate(embed_refs):
        parts = ref.shape[0] // 256
        for part in range(parts):
            rows = dot(mixer, ref[part * 256 : (part + 1) * 256, :]).astype(BF)
            base = pl.multiple_of((block_ref[piece] * parts + part) * 128, 128)
            low_ref[pl.ds(base, 128), :] = rows[:128]
            high[pl.ds(base, 128), :] = rows[128:]
    token_ref[...] = dot(patch[...], high[...], 0, 0)


def store_patch(patch, out, splitter):
    even, odd = split_time(out, splitter)
    even, odd = even.astype(BF), odd.astype(BF)
    for block in range(out.shape[0] // 64):
        here = slice(block * 64, (block + 1) * 64)
        patch[block * 128 : block * 128 + 64, :] = even[here]
        patch[block * 128 + 64 : (block + 1) * 128, :] = odd[here]


def back_kernel(
    got_ref, first_ref, second_ref, token_ref, low_ref, k1_ref, k2_ref, active_ref,
    out_ref, all1, all2, patch, *, channels, middle
):
    splitter = split_matrix()
    odd = got_ref[channels : 2 * channels, :].astype(F32)
    all1[:channels, :] = later(odd).astype(BF)
    all1[channels:, :] = got_ref[: 2 * channels, :]
    even, odd = split_time(got_ref[2 * channels :, :], splitter)
    store_taps(all2, 0, even, odd)
    first = silu(first_ref[...] + dot(k1_ref[: 3 * channels, :], all1[...], 0, 0)).astype(BF)
    even, odd = split_time(first, splitter)
    store_taps(all2, 3 * middle, even, odd)
    out = silu(second_ref[...] + dot(k2_ref[: 6 * middle, :], all2[...], 0, 0)).astype(BF)
    store_patch(patch, out, splitter)
    total = token_ref[...] + dot(patch[...], low_ref[...], 0, 0)
    count, width = total.shape
    out_ref[:count, :] = total.astype(BF)
    tail = jnp.broadcast_to(active_ref[...].astype(F32), (EXTRA, count))
    tail = jnp.concatenate([tail, jnp.zeros((EXTRA, width - count), F32)], axis=1)
    out_ref[count:, :] = tail.astype(BF)


def normal(tokens):
    value = tokens.astype(F32)
    value = value - jnp.mean(value, axis=-1, keepdims=True)
    spread = jnp.mean(value * value, axis=-1, keepdims=True)
    return (value * lax.rsqrt(spread + epsilon)).astype(BF)


def lift(chunk_refs, project, normed, keys, values):
    width = project.shape[0]
    for slot, ref in enumerate(chunk_refs):
        count = ref.shape[0] - EXTRA
        normed[slot * count : (slot + 1) * count, :] = normal(ref[:count, :])
    rows = normed[...]
    keys[...] = dot(rows, project[:, width : 2 * width]).astype(BF)
    values[...] = dot(rows, project[:, 2 * width :]).astype(BF)


def collect(block_ref, pieces_refs, target, sems):
    copies = []
    for piece, ref in enumerate(pieces_refs):
        depth = ref.shape[0]
        base = pl.multiple_of(block_ref[piece] * depth, depth)
        copies.append(pltpu.make_async_copy(ref, target.at[pl.ds(base, depth), :], sems.at[piece]))
        copies[-1].start()
    return copies


def prepare_kernel(block_ref, place_ref, order_ref, *refs, pieces, chunks, count):
    project_refs = refs[:pieces]
    chunk_refs = refs[pieces : pieces + chunks]
    project, normed, keys, values, perm_ref, sems = refs[pieces + chunks :]
    copies = collect(block_ref, project_refs, project, sems)
    shards = order_ref.shape[0]
    square = iota((count, count), 0) == iota((count, count), 1)
    lane = iota((1, count), 1)
    labels = jnp.concatenate([lane + place_ref[slot] * count for slot in range(shards)], axis=1)
    labels = labels.astype(F32)
    for slot in range(shards):
        row = order_ref[pl.ds(place_ref[slot], 1), :].astype(F32)
        across = jnp.broadcast_to(row, (count, count))
        down = jnp.sum(jnp.where(square, across, 0.0), axis=1, keepdims=True)
        perm_ref[slot * count : (slot + 1) * count, :] = one_hot(labels == down)
    for copy in copies:
        copy.wait()
    lift(chunk_refs, project, normed, keys, values)


def finish_kernel(block_ref, place_ref, perm_ref, project, normed0, keys0, values0, *refs, pieces, chunks, early, count):
    chunk_refs = refs[:chunks]
    output_refs = refs[chunks : chunks + pieces]
    out_ref, output, normed1, keys1, values1, cap, mixed, sems = refs[chunks + pieces :]
    copies = collect(block_ref, output_refs, output, sems)
    width = project.shape[0]
    lift(chunk_refs[early:], project, normed1, keys1, values1)
    near = early * count
    own = perm_ref[pl.ds(pl.multiple_of(place_ref[chunks] * count, count), count), :]
    picked = (dot(own[:, :near], normed0[...]) + dot(own[:, near:], normed1[...])).astype(BF)
    head = width // HEADS
    queries = (dot(picked, project[:, :width]) * head ** (-0.5)).astype(BF)
    on = None
    token = None
    for slot, ref in enumerate(chunk_refs):
        here = slice(slot * count, (slot + 1) * count)
        term = dot(ref[count:, :count], perm_ref[here, :])
        on = term if on is None else on + term
        term = dot(own[:, here], ref[:count, :])
        token = term if token is None else token + term
    allowed = (own.astype(F32) + jnp.broadcast_to(on[:1], own.shape)) > 0.5
    cap[...] = jnp.where(allowed, largest, masked_score)
    low = iota((count, 2 * head), 1) < head
    for pair in range(HEADS // 2):
        here = slice(pair * 2 * head, (pair + 1) * 2 * head)
        query = queries[:, here]
        zero = jnp.zeros_like(query)
        both = jnp.concatenate([jnp.where(low, query, zero), jnp.where(low, zero, query)], axis=0)
        scores = jnp.concatenate([dot(both, keys0[:, here], 1, 1), dot(both, keys1[:, here], 1, 1)], axis=1)
        weights, scale = [], []
        for half in range(2):
            score = jnp.minimum(scores[half * count : (half + 1) * count], cap[...])
            weight = jnp.exp(score - jnp.max(score, axis=-1, keepdims=True))
            scale.append(1.0 / jnp.sum(weight, axis=-1, keepdims=True))
            weights.append(weight.astype(BF))
        weights = jnp.concatenate(weights, axis=0)
        part = dot(weights[:, :near], values0[:, here]) + dot(weights[:, near:], values1[:, here])
        mixed[:, here] = jnp.where(low, part[:count] * scale[0], part[count:] * scale[1]).astype(BF)
    for copy in copies:
        copy.wait()
    out_ref[...] = (token + dot(mixed[...], output[...])).astype(BF)


def vmem():
    return pl.BlockSpec(memory_space=pltpu.VMEM)


def smem():
    return pl.BlockSpec(memory_space=pltpu.SMEM)


def hbm():
    return pl.BlockSpec(memory_space=pl.ANY)


def params(mib):
    return pltpu.CompilerParams(vmem_limit_bytes=mib * 1024 * 1024)


def array(shape, dtype=BF):
    return jax.ShapeDtypeStruct(shape, dtype)


def front(rows, k1, wires):
    channels = rows.shape[0] // wires
    middle = k1.shape[1]
    length = rows.shape[1] // 2
    return pl.pallas_call(
        functools.partial(front_kernel, wires=wires, channels=channels, middle=middle),
        out_shape=(
            array((2 * channels + middle, length)),
            array((6 * channels, length)),
            array(((wires // 2 - 1) * 3 * middle, length // 2)),
        ),
        in_specs=[vmem()] * 2,
        out_specs=[vmem()] * 3,
        scratch_shapes=[pltpu.VMEM((wires * 3 * channels, length), BF)],
        compiler_params=params(12),
        name="front",
    )(rows, k1)


def central(blocks, taps1, taps2, k1, k2, embeds, count):
    middle, outer = k1.shape[1], k2.shape[1]
    channels = k1.shape[0] // 9
    width = embeds[0].shape[1]
    return pl.pallas_call(
        functools.partial(middle_kernel, channels=channels, middle=middle, pieces=len(embeds)),
        out_shape=(
            array((middle, taps1.shape[1]), F32),
            array((outer, taps2.shape[1]), F32),
            array((count, width), F32),
            array((2 * outer, width)),
        ),
        in_specs=[smem()] + [vmem()] * (4 + len(embeds)),
        out_specs=[vmem()] * 4,
        scratch_shapes=[pltpu.VMEM((2 * outer, width), BF), pltpu.VMEM((2 * outer, count), BF)],
        compiler_params=params(12),
        name="central",
    )(blocks, taps1, taps2, k1, k2, *embeds)


def back(got, parts, k1, k2, active):
    middle = k1.shape[1]
    channels = k1.shape[0] // 9
    length = got.shape[1]
    count = active.shape[1]
    width = parts[-1].shape[1]
    return pl.pallas_call(
        functools.partial(back_kernel, channels=channels, middle=middle),
        out_shape=array((count + EXTRA, width)),
        in_specs=[vmem()] * (4 + len(parts)),
        out_specs=vmem(),
        scratch_shapes=[
            pltpu.VMEM((3 * channels, length), BF),
            pltpu.VMEM((6 * middle, length // 2), BF),
            pltpu.VMEM((2 * k2.shape[1], count), BF),
        ],
        compiler_params=params(12),
        name="back",
    )(got, *parts, k1, k2, active)


def prepare(blocks, places, order, projects, chunks):
    shards, count = order.shape
    width = chunks[0].shape[1]
    size, near = shards * count, len(chunks) * count
    return pl.pallas_call(
        functools.partial(prepare_kernel, pieces=len(projects), chunks=len(chunks), count=count),
        out_shape=(array((width, 3 * width)),) + (array((near, width)),) * 3 + (array((size, size)),),
        in_specs=[smem()] * 2 + [vmem()] + [hbm()] * len(projects) + [vmem()] * len(chunks),
        out_specs=[vmem()] * 5,
        scratch_shapes=[pltpu.SemaphoreType.DMA((len(projects),))],
        compiler_params=params(8 + size // 128),
        name="prepare",
    )(blocks, places, order, *projects, *chunks)


def finish(blocks, places, ready, chunks, outputs, early):
    project, normed, keys, values, perm = ready
    width = project.shape[0]
    size = perm.shape[0]
    count = size // len(chunks)
    far = size - early * count
    return pl.pallas_call(
        functools.partial(finish_kernel, pieces=len(outputs), chunks=len(chunks), early=early, count=count),
        out_shape=array((count, width)),
        in_specs=[smem()] * 2 + [vmem()] * (5 + len(chunks)) + [hbm()] * len(outputs),
        out_specs=vmem(),
        scratch_shapes=[
            pltpu.VMEM((width, width), BF),
            pltpu.VMEM((far, width), BF),
            pltpu.VMEM((far, width), BF),
            pltpu.VMEM((far, width), BF),
            pltpu.VMEM((count, size), F32),
            pltpu.VMEM((count, width), BF),
            pltpu.SemaphoreType.DMA((len(outputs),)),
        ],
        compiler_params=params(8 + size // 64),
        name="finish",
    )(blocks, places, perm, project, normed, keys, values, *chunks, *outputs)


def exchanged(value, axis, flip):
    count = lax.axis_size(axis)
    return lax.ppermute(value, axis, [(i, i ^ flip) for i in range(count)])


def paired():
    return lax.axis_size("mp") == 2 and lax.axis_size("section") == 2


def gathered(weight):
    if paired():
        across = exchanged(weight, "mp", 1)
        beside = exchanged(weight, "section", 1)
        return [weight, beside, across, exchanged(across, "section", 1)]
    return [lax.all_gather(weight, ("mp", "section"), axis=0, tiled=True)]


def layer(
    readout, first_kernel, second_kernel, embed_weight, project_weight, output_weight, order, active
):
    shards = lax.axis_size("seq")
    position = lax.axis_index("seq").astype(jnp.int32)
    embeds = gathered(embed_weight)
    projects = gathered(project_weight)
    outputs = gathered(output_weight)
    pieces = len(embeds)
    own = lax.axis_index("mp") * 2 + lax.axis_index("section") if pieces > 1 else 0
    blocks = jnp.arange(pieces, dtype=jnp.int32) ^ own
    channels, wires, ticks = readout.shape[1:]
    k1 = first_kernel.reshape(-1, first_kernel.shape[-1])
    k2 = second_kernel.reshape(-1, second_kernel.shape[-1])
    order = order.reshape(shards, -1)
    count = order.shape[1]
    slots = jnp.arange(shards, dtype=jnp.int32)
    msg, taps1, taps2 = front(readout.reshape(channels * wires, ticks), k1, wires)
    got = lax.ppermute(msg, "seq", [(i, i + 1) for i in range(shards - 1)])
    parts = central(blocks, taps1, taps2, k1, k2, embeds, count)
    tokens = back(got, parts, k1, k2, active)
    if shards == 4:
        slot = jnp.zeros((1,), jnp.int32)
        places = slots ^ position
        chunks = [tokens] + [exchanged(tokens, "seq", flip) for flip in (1, 2, 3)]
    else:
        slot = position.reshape(1)
        places = slots
        everyone = lax.all_gather(tokens, "seq", axis=0, tiled=True)
        chunks = [everyone[i * (count + EXTRA) : (i + 1) * (count + EXTRA)] for i in range(shards)]
    early = shards // 2
    places = jnp.concatenate([places, slot])
    ready = prepare(blocks, places, order, projects, chunks[:early])
    result = finish(blocks, places, ready, chunks, outputs, early)
    return result[None]


def solution(mesh):
    in_specs = (
        P(("groups", "mp", "section"), None, "seq", None),
        P(),
        P(),
        P(("mp", "section"), None),
        P(("mp", "section"), None),
        P(("mp", "section"), None),
        P(("groups", "mp", "section"), None),
        P(("groups", "mp", "section"), "seq"),
    )
    out_specs = P(("groups", "mp", "section"), "seq", None)
    return jax.shard_map(layer, mesh=mesh, in_specs=in_specs, out_specs=out_specs, check_vma=False)
```

time: 87.4 us -> 85.2 us (0.975)
  the two profiles are of different devices: /device:TPU:0 before, /device:TPU:8 now
where the time goes in v2:
time: 85.2 us; the launch traced here: 84.5 us
  waiting for transfers between devices  41.6 us (49%)
  Pallas kernels  16.5 us (19%)
  local copies, waits for them, and re-layouts  14.3 us (17%)
  starting transfers between devices  11.9 us (14%)
    ppermute x12, waiting for transfers between devices, exchanged(): return lax.ppermute(value, axis, [(i, i ^ flip) for i in range(count)])  41.6 us
    unnamed x40, local copies, waits for them, and re-layouts  14.3 us
    ppermute x12, starting transfers between devices, exchanged(): return lax.ppermute(value, axis, [(i, i ^ flip) for i in range(count)])  8.45 us
    pallas_call x1, Pallas kernels, finish(): pl.pallas_call(functools.partial(finish_kernel, pieces=len(outputs), chun...  6.13 us
    ppermute x1, starting transfers between devices, layer(): got = lax.ppermute(msg, 'seq', [(i, i + 1) for i in range(shards - 1)])  3.48 us
    pallas_call x1, Pallas kernels, prepare(): pl.pallas_call(functools.partial(prepare_kernel, pieces=len(projects), ch...  3.32 us
    pallas_call x1, Pallas kernels, central(): pl.pallas_call(functools.partial(middle_kernel, channels=channels, middle...  2.64 us
    pallas_call x1, Pallas kernels, front(): pl.pallas_call(functools.partial(front_kernel, wires=wires, channels=chan...  2.28 us
  transfers between devices with their start and end apart: 13, of which 5 were waited for; matrix products, arithmetic and copies ran while one was open for 0% of the time, Pallas kernels for 12%

profile of v2, /device:TPU:8, one launch (start us, length us, event | category | flops | bytes accessed | tf_op | source)
XLA Modules:
  0.0 84.5 jit_solution(7318959749893235936)
XLA Ops:
  0.0 1.5 %collective-permute-start.1 = (bf16[192,2304]{1,0:T(8,128)(2,1)}, bf16[192,2304]{1,0:T(8,128)(2,1)S(1)}, u32[]{:S(2)}, u32[]{:S(2)}) collective-permute-start(bf16[192,2304]{1,0:T(8,128)(2,1)} %refs_0_.3), channel_id=1, source_target_pairs={{0,2},{2,0},{1,3},{3,1},{4,6},{6,4},{5,7},{7,5},{8,10},{10,8},{9,1... | collective-permute-start | bytes 2654216 | tf_op jit(solution)/shard_map/ppermute | solution.py:359
  2.5 20.2 %collective-permute-done.1.refs_2_ = bf16[192,2304]{1,0:T(8,128)(2,1)S(1)} collective-permute-done((bf16[192,2304]{1,0:T(8,128)(2,1)}, bf16[192,2304]{1,0:T(8,128)(2,1)S(1)}, u32[]{:S(2)}, u32[]{:S(2)}) %collective-permute-start.1) | collective-permute-done | bytes 884768 | tf_op jit(solution)/shard_map/ppermute | solution.py:359
  22.7 7.3 %collective-permute-done.5.refs_2_ = bf16[256,768]{1,0:T(8,128)(2,1)S(1)} collective-permute-done((bf16[256,768]{1,0:T(8,128)(2,1)}, bf16[256,768]{1,0:T(8,128)(2,1)S(1)}, u32[]{:S(2)}, u32[]{:S(2)}) %collective-permute-start.5) | collective-permute-done | bytes 393248 | tf_op jit(solution)/shard_map/ppermute | solution.py:359
  30.0 1.1 %copy-done.2 = bf16[3,3,64,128]{3,2,1,0:T(8,128)(2,1)S(1)} copy-done((bf16[3,3,64,128]{3,2,1,0:T(8,128)(2,1)S(1)}, bf16[3,3,64,128]{3,2,1,0:T(8,128)(2,1)}, u32[]{:S(2)}) %copy-start.2) | copy-done | bytes 147480
  31.1 1.2 %copy-done.4 = bf16[1,64,8,1024]{3,2,1,0:T(8,128)(2,1)S(1)} copy-done((bf16[1,64,8,1024]{3,2,1,0:T(8,128)(2,1)S(1)}, bf16[1,64,8,1024]{3,2,1,0:T(8,128)(2,1)}, u32[]{:S(2)}) %copy-start.4) | copy-done | bytes 1048600
  32.3 2.3 %front.1 = (bf16[256,512]{1,0:T(8,128)(2,1)}, bf16[384,512]{1,0:T(8,128)(2,1)S(1)}, bf16[1152,256]{1,0:T(8,128)(2,1)S(1)}) custom-call(bf16[512,1024]{1,0:T(8,128)(2,1)S(1)} %bitcast.10, bf16[576,128]{1,0:T(8,128)(2,1)S(1)} %bitcast.7), custom_call_target="tpu_custom_call" | custom-call | tf_op jit(solution)/shard_map/front/pallas_call | solution.py:261
  36.2 3.5 %collective-permute-start.3 = (bf16[256,512]{1,0:T(8,128)(2,1)}, bf16[256,512]{1,0:T(8,128)(2,1)}, u32[]{:S(2)}, u32[]{:S(2)}) collective-permute-start(bf16[256,512]{1,0:T(8,128)(2,1)} %get-tuple-element.17), channel_id=1, source_target_pairs={{0,4},{4,8},{8,12},{1,5},{5,9},{9,13},{2,6},{6,10},{10,14},{3,7},{... | collective-permute-start | bytes 786440 | tf_op jit(solution)/shard_map/ppermute | solution.py:392
  40.4 1.5 %collective-permute-start.11 = (bf16[192,768]{1,0:T(8,128)(2,1)}, bf16[192,768]{1,0:T(8,128)(2,1)}, u32[]{:S(2)}, u32[]{:S(2)}) collective-permute-start(bf16[192,768]{1,0:T(8,128)(2,1)} %refs_4_.1), channel_id=1, source_target_pairs={{0,2},{2,0},{1,3},{3,1},{4,6},{6,4},{5,7},{7,5},{8,10},{10,8},{9,1... | collective-permute-start | bytes 884744 | tf_op jit(solution)/shard_map/ppermute | solution.py:359
  42.0 1.1 %copy-done = bf16[3,3,128,256]{3,2,1,0:T(8,128)(2,1)S(1)} copy-done((bf16[3,3,128,256]{3,2,1,0:T(8,128)(2,1)S(1)}, bf16[3,3,128,256]{3,2,1,0:T(8,128)(2,1)}, u32[]{:S(2)}) %copy-start) | copy-done | bytes 589848
  43.9 1.1 %copy-done.7 = bf16[1152,256]{1,0:T(8,128)(2,1)S(1)} copy-done((bf16[1152,256]{1,0:T(8,128)(2,1)S(1)}, bf16[1152,256]{1,0:T(8,128)(2,1)}, u32[]{:S(2)}) %copy-start.7) | copy-done | bytes 589848
  45.0 1.0 %copy-done.8 = bf16[256,768]{1,0:T(8,128)(2,1)S(1)} copy-done((bf16[256,768]{1,0:T(8,128)(2,1)S(1)}, bf16[256,768]{1,0:T(8,128)(2,1)}, u32[]{:S(2)}) %copy-start.8) | copy-done | bytes 393240
  46.0 1.0 %copy-done.10 = bf16[256,768]{1,0:T(8,128)(2,1)S(1)} copy-done((bf16[256,768]{1,0:T(8,128)(2,1)S(1)}, bf16[256,768]{1,0:T(8,128)(2,1)}, u32[]{:S(2)}) %copy-start.10) | copy-done | bytes 393240
  47.0 1.0 %copy-done.12 = bf16[256,768]{1,0:T(8,128)(2,1)S(1)} copy-done((bf16[256,768]{1,0:T(8,128)(2,1)S(1)}, bf16[256,768]{1,0:T(8,128)(2,1)}, u32[]{:S(2)}) %copy-start.12) | copy-done | bytes 393240
  48.0 1.0 %copy-done.14 = bf16[384,512]{1,0:T(8,128)(2,1)S(1)} copy-done((bf16[384,512]{1,0:T(8,128)(2,1)S(1)}, bf16[384,512]{1,0:T(8,128)(2,1)}, u32[]{:S(2)}) %copy-start.14) | copy-done | bytes 393240
  49.0 2.6 %central.1 = (f32[128,512]{1,0:T(8,128)S(1)}, f32[256,256]{1,0:T(8,128)S(1)}, f32[128,768]{1,0:T(8,128)S(1)}, bf16[512,768]{1,0:T(8,128)(2,1)S(1)}) custom-call(s32[4]{0:T(128)S(1)} %iota_xor_fusion.1.block_ref, bf16[384,512]{1,0:T(8,128)(2,1)S(1)} %copy-done.14, bf16[1152,256]{1,0:T(8,128)(2,1)S(1)} %copy-done.7, bf16[576,128]{1,0:T(8,128)(2,1)S(1)} %bitcast.8, ...), custom_call_target="tpu_custom_call" | custom-call | tf_op jit(solution)/shard_map/central/pallas_call | solution.py:280
  51.6 2.1 %back.1.refs_4_.refs_0_ = bf16[136,768]{1,0:T(8,128)(2,1)S(1)} custom-call(bf16[256,512]{1,0:T(8,128)(2,1)} %collective-permute-done.3.got_ref, f32[128,512]{1,0:T(8,128)S(1)} %get-tuple-element.20.first_ref, f32[256,256]{1,0:T(8,128)S(1)} %get-tuple-element.21.second_ref, f32[128,768]{1,0:T(8,128)S(1)} %get-tuple-element.22.token_ref, ...), custom_call_target="tpu_custom_call" | custom-call | tf_op jit(solution)/shard_map/back/pallas_call | solution.py:302
  53.8 1.2 %collective-permute-start.7 = (bf16[136,768]{1,0:T(8,128)(2,1)S(1)}, bf16[136,768]{1,0:T(8,128)(2,1)S(1)}, u32[]{:S(2)}, u32[]{:S(2)}) collective-permute-start(bf16[136,768]{1,0:T(8,128)(2,1)S(1)} %back.1.refs_4_.refs_0_), channel_id=1, source_target_pairs={{0,4},{4,0},{8,12},{12,8},{1,5},{5,1},{9,13},{13,9},{2,6},{6,2},{1... | collective-permute-start | bytes 626696 | tf_op jit(solution)/shard_map/ppermute | solution.py:359
  55.5 1.9 %collective-permute-start.8 = (bf16[136,768]{1,0:T(8,128)(2,1)S(1)}, bf16[136,768]{1,0:T(8,128)(2,1)S(1)}, u32[]{:S(2)}, u32[]{:S(2)}) collective-permute-start(bf16[136,768]{1,0:T(8,128)(2,1)S(1)} %back.1.refs_4_.refs_0_), channel_id=1, source_target_pairs={{0,8},{4,12},{8,0},{12,4},{1,9},{5,13},{9,1},{13,5},{2,10},{6,14},... | collective-permute-start | bytes 626696 | tf_op jit(solution)/shard_map/ppermute | solution.py:359
  57.4 5.3 %collective-permute-done.7.refs_5_.refs_1_ = bf16[136,768]{1,0:T(8,128)(2,1)S(1)} collective-permute-done((bf16[136,768]{1,0:T(8,128)(2,1)S(1)}, bf16[136,768]{1,0:T(8,128)(2,1)S(1)}, u32[]{:S(2)}, u32[]{:S(2)}) %collective-permute-start.7) | collective-permute-done | bytes 208928 | tf_op jit(solution)/shard_map/ppermute | solution.py:359
  63.6 3.3 %prepare.1 = (bf16[768,2304]{1,0:T(8,128)(2,1)S(1)}, bf16[256,768]{1,0:T(8,128)(2,1)S(1)}, bf16[256,768]{1,0:T(8,128)(2,1)S(1)}, bf16[256,768]{1,0:T(8,128)(2,1)S(1)}, bf16[512,512]{1,0:T(8,128)(2,1)S(1)}) custom-call(s32[4]{0:T(128)S(1)} %iota_xor_fusion.1.block_ref, s32[5]{0:T(128)S(1)} %pad_add_fusion.place_ref, s32[4,128]{1,0:T(4,128)S(1)} %bitcast.11, ...), custom_call_target="tpu_custom_call" | custom-call | tf_op jit(solution)/shard_map/prepare/pallas_call | solution.py:321
  67.6 4.3 %collective-permute-done.8.refs_2_ = bf16[136,768]{1,0:T(8,128)(2,1)S(1)} collective-permute-done((bf16[136,768]{1,0:T(8,128)(2,1)S(1)}, bf16[136,768]{1,0:T(8,128)(2,1)S(1)}, u32[]{:S(2)}, u32[]{:S(2)}) %collective-permute-start.8) | collective-permute-done | bytes 208928 | tf_op jit(solution)/shard_map/ppermute | solution.py:359
  71.9 4.5 %collective-permute-done.9.refs_3_ = bf16[136,768]{1,0:T(8,128)(2,1)S(1)} collective-permute-done((bf16[136,768]{1,0:T(8,128)(2,1)S(1)}, bf16[136,768]{1,0:T(8,128)(2,1)S(1)}, u32[]{:S(2)}, u32[]{:S(2)}) %collective-permute-start.9) | collective-permute-done | bytes 208928 | tf_op jit(solution)/shard_map/ppermute | solution.py:359
  76.5 1.0 %copy-done.15 = bf16[192,768]{1,0:T(8,128)(2,1)S(1)} copy-done((bf16[192,768]{1,0:T(8,128)(2,1)S(1)}, bf16[192,768]{1,0:T(8,128)(2,1)}, u32[]{:S(2)}) %copy-start.15) | copy-done | bytes 294936
  78.4 6.1 %finish.1 = bf16[128,768]{1,0:T(8,128)(2,1)} custom-call(s32[4]{0:T(128)S(1)} %iota_xor_fusion.1.block_ref, s32[5]{0:T(128)S(1)} %pad_add_fusion.place_ref, bf16[512,512]{1,0:T(8,128)(2,1)S(1)} %get-tuple-element.24.perm_ref, bf16[768,2304]{1,0:T(8,128)(2,1)S(1)} %get-tuple-element.25.project, bf16[256,768]{1,0:T(8,128)(2,1)S(1)} %get-tuple-element.26.normed0, ...), custom_call_target="tpu_custom_call" | custom-call | tf_op jit(solution)/shard_map/finish/pallas_call | solution.py:338
  (50 shorter events, 7.4 us)
Async XLA Ops:
  0.0 51.6 %copy-start.1 = (bf16[3,3,128,256]{3,2,1,0:T(8,128)(2,1)S(1)}, bf16[3,3,128,256]{3,2,1,0:T(8,128)(2,1)}, u32[]{:S(2)}) copy-start(bf16[3,3,128,256]{3,2,1,0:T(8,128)(2,1)} %param.10) | copy-start | bytes 1769476
  0.0 22.7 %collective-permute-start.1 = (bf16[192,2304]{1,0:T(8,128)(2,1)}, bf16[192,2304]{1,0:T(8,128)(2,1)S(1)}, u32[]{:S(2)}, u32[]{:S(2)}) collective-permute-start(bf16[192,2304]{1,0:T(8,128)(2,1)} %refs_0_.3), channel_id=1, source_target_pairs={{0,2},{2,0},{1,3},{3,1},{4,6},{6,4},{5,7},{7,5},{8,10},{10,8},{9,1... | collective-permute-start | bytes 2654216 | tf_op jit(solution)/shard_map/ppermute | solution.py:359
  1.5 28.5 %collective-permute-start.5 = (bf16[256,768]{1,0:T(8,128)(2,1)}, bf16[256,768]{1,0:T(8,128)(2,1)S(1)}, u32[]{:S(2)}, u32[]{:S(2)}) collective-permute-start(bf16[256,768]{1,0:T(8,128)(2,1)} %refs_0_.2), channel_id=1, source_target_pairs={{0,2},{2,0},{1,3},{3,1},{4,6},{6,4},{5,7},{7,5},{8,10},{10,8},{9,1... | collective-permute-start | bytes 1179656 | tf_op jit(solution)/shard_map/ppermute | solution.py:359
  2.0 53.5 %collective-permute-start = (bf16[192,2304]{1,0:T(8,128)(2,1)}, bf16[192,2304]{1,0:T(8,128)(2,1)S(1)}, u32[]{:S(2)}, u32[]{:S(2)}) collective-permute-start(bf16[192,2304]{1,0:T(8,128)(2,1)} %refs_0_.3), channel_id=1, source_target_pairs={{0,1},{1,0},{2,3},{3,2},{4,5},{5,4},{6,7},{7,6},{8,9},{9,8},{10,11... | collective-permute-start | bytes 2654216 | tf_op jit(solution)/shard_map/ppermute | solution.py:359
  2.0 37.7 %collective-permute-start.4 = (bf16[256,768]{1,0:T(8,128)(2,1)}, bf16[256,768]{1,0:T(8,128)(2,1)S(1)}, u32[]{:S(2)}, u32[]{:S(2)}) collective-permute-start(bf16[256,768]{1,0:T(8,128)(2,1)} %refs_0_.2), channel_id=1, source_target_pairs={{0,1},{1,0},{2,3},{3,2},{4,5},{5,4},{6,7},{7,6},{8,9},{9,8},{10,11... | collective-permute-start | bytes 1179656 | tf_op jit(solution)/shard_map/ppermute | solution.py:359
  22.7 40.8 %collective-permute-start.2 = (bf16[192,2304]{1,0:T(8,128)(2,1)S(1)}, bf16[192,2304]{1,0:T(8,128)(2,1)}, u32[]{:S(2)}, u32[]{:S(2)}) collective-permute-start(bf16[192,2304]{1,0:T(8,128)(2,1)S(1)} %collective-permute-done.1.refs_2_), channel_id=1, source_target_pairs={{0,1},{1,0},{2,3},{3,2},{4,5},{5,4},{6,7},{7,6},{8,9},{9,8},{10,11... | collective-permute-start | bytes 2654216 | tf_op jit(solution)/shard_map/ppermute | solution.py:359
  30.0 11.9 %copy-start.9 = (bf16[256,768]{1,0:T(8,128)(2,1)}, bf16[256,768]{1,0:T(8,128)(2,1)S(1)}, u32[]{:S(2)}) copy-start(bf16[256,768]{1,0:T(8,128)(2,1)S(1)} %collective-permute-done.5.refs_2_) | copy-start | bytes 1179652
  30.0 11.9 %collective-permute-start.6 = (bf16[256,768]{1,0:T(8,128)(2,1)S(1)}, bf16[256,768]{1,0:T(8,128)(2,1)}, u32[]{:S(2)}, u32[]{:S(2)}) collective-permute-start(bf16[256,768]{1,0:T(8,128)(2,1)S(1)} %collective-permute-done.5.refs_2_), channel_id=1, source_target_pairs={{0,1},{1,0},{2,3},{3,2},{4,5},{5,4},{6,7},{7,6},{8,9},{9,8},{10,11... | collective-permute-start | bytes 1179656 | tf_op jit(solution)/shard_map/ppermute | solution.py:359
  30.0 1.1 %copy-start.2 = (bf16[3,3,64,128]{3,2,1,0:T(8,128)(2,1)S(1)}, bf16[3,3,64,128]{3,2,1,0:T(8,128)(2,1)}, u32[]{:S(2)}) copy-start(bf16[3,3,64,128]{3,2,1,0:T(8,128)(2,1)} %param.9) | copy-start | bytes 442372
  31.1 1.2 %copy-start.4 = (bf16[1,64,8,1024]{3,2,1,0:T(8,128)(2,1)S(1)}, bf16[1,64,8,1024]{3,2,1,0:T(8,128)(2,1)}, u32[]{:S(2)}) copy-start(bf16[1,64,8,1024]{3,2,1,0:T(8,128)(2,1)} %param.8) | copy-start | bytes 3145732
  32.3 19.3 %copy-start.19 = (s32[1,128]{1,0:T(1,128)S(1)}, s32[1,128]{1,0:T(1,128)}, u32[]{:S(2)}) copy-start(s32[1,128]{1,0:T(1,128)} %active_ref.1) | copy-start | bytes 1540
  32.3 31.2 %copy-start.18 = (s32[1,512]{1,0:T(1,128)S(1)}, s32[1,512]{1,0:T(1,128)}, u32[]{:S(2)}) copy-start(s32[1,512]{1,0:T(1,128)} %param.14) | copy-start | bytes 6148
  36.2 15.4 %collective-permute-start.3 = (bf16[256,512]{1,0:T(8,128)(2,1)}, bf16[256,512]{1,0:T(8,128)(2,1)}, u32[]{:S(2)}, u32[]{:S(2)}) collective-permute-start(bf16[256,512]{1,0:T(8,128)(2,1)} %get-tuple-element.17), channel_id=1, source_target_pairs={{0,4},{4,8},{8,12},{1,5},{5,9},{9,13},{2,6},{6,10},{10,14},{3,7},{... | collective-permute-start | bytes 786440 | tf_op jit(solution)/shard_map/ppermute | solution.py:392
  40.4 14.5 %collective-permute-start.11 = (bf16[192,768]{1,0:T(8,128)(2,1)}, bf16[192,768]{1,0:T(8,128)(2,1)}, u32[]{:S(2)}, u32[]{:S(2)}) collective-permute-start(bf16[192,768]{1,0:T(8,128)(2,1)} %refs_4_.1), channel_id=1, source_target_pairs={{0,2},{2,0},{1,3},{3,1},{4,6},{6,4},{5,7},{7,5},{8,10},{10,8},{9,1... | collective-permute-start | bytes 884744 | tf_op jit(solution)/shard_map/ppermute | solution.py:359
  41.9 1.1 %copy-start = (bf16[3,3,128,256]{3,2,1,0:T(8,128)(2,1)S(1)}, bf16[3,3,128,256]{3,2,1,0:T(8,128)(2,1)}, u32[]{:S(2)}) copy-start(bf16[3,3,128,256]{3,2,1,0:T(8,128)(2,1)} %param.10) | copy-start | bytes 1769476
  43.9 1.1 %copy-start.7 = (bf16[1152,256]{1,0:T(8,128)(2,1)S(1)}, bf16[1152,256]{1,0:T(8,128)(2,1)}, u32[]{:S(2)}) copy-start(bf16[1152,256]{1,0:T(8,128)(2,1)} %copy-done.6) | copy-start | bytes 1769476
  45.0 1.0 %copy-start.8 = (bf16[256,768]{1,0:T(8,128)(2,1)S(1)}, bf16[256,768]{1,0:T(8,128)(2,1)}, u32[]{:S(2)}) copy-start(bf16[256,768]{1,0:T(8,128)(2,1)} %refs_0_.2) | copy-start | bytes 1179652
  46.0 1.0 %copy-start.10 = (bf16[256,768]{1,0:T(8,128)(2,1)S(1)}, bf16[256,768]{1,0:T(8,128)(2,1)}, u32[]{:S(2)}) copy-start(bf16[256,768]{1,0:T(8,128)(2,1)} %copy-done.9) | copy-start | bytes 1179652
  49.0 14.6 %copy-start.5 = (bf16[192,2304]{1,0:T(8,128)(2,1)S(1)}, bf16[192,2304]{1,0:T(8,128)(2,1)}, u32[]{:S(2)}) copy-start(bf16[192,2304]{1,0:T(8,128)(2,1)} %refs_0_.3) | copy-start | bytes 2654212
  53.8 8.9 %collective-permute-start.7 = (bf16[136,768]{1,0:T(8,128)(2,1)S(1)}, bf16[136,768]{1,0:T(8,128)(2,1)S(1)}, u32[]{:S(2)}, u32[]{:S(2)}) collective-permute-start(bf16[136,768]{1,0:T(8,128)(2,1)S(1)} %back.1.refs_4_.refs_0_), channel_id=1, source_target_pairs={{0,4},{4,0},{8,12},{12,8},{1,5},{5,1},{9,13},{13,9},{2,6},{6,2},{1... | collective-permute-start | bytes 626696 | tf_op jit(solution)/shard_map/ppermute | solution.py:359
  55.0 11.9 %collective-permute-start.10 = (bf16[192,768]{1,0:T(8,128)(2,1)}, bf16[192,768]{1,0:T(8,128)(2,1)S(1)}, u32[]{:S(2)}, u32[]{:S(2)}) collective-permute-start(bf16[192,768]{1,0:T(8,128)(2,1)} %refs_4_.1), channel_id=1, source_target_pairs={{0,1},{1,0},{2,3},{3,2},{4,5},{5,4},{6,7},{7,6},{8,9},{9,8},{10,11... | collective-permute-start | bytes 884744 | tf_op jit(solution)/shard_map/ppermute | solution.py:359
  55.0 12.6 %collective-permute-start.12 = (bf16[192,768]{1,0:T(8,128)(2,1)}, bf16[192,768]{1,0:T(8,128)(2,1)}, u32[]{:S(2)}, u32[]{:S(2)}) collective-permute-start(bf16[192,768]{1,0:T(8,128)(2,1)} %collective-permute-done.11.refs_6_), channel_id=1, source_target_pairs={{0,1},{1,0},{2,3},{3,2},{4,5},{5,4},{6,7},{7,6},{8,9},{9,8},{10,11... | collective-permute-start | bytes 884744 | tf_op jit(solution)/shard_map/ppermute | solution.py:359
  55.5 16.4 %collective-permute-start.8 = (bf16[136,768]{1,0:T(8,128)(2,1)S(1)}, bf16[136,768]{1,0:T(8,128)(2,1)S(1)}, u32[]{:S(2)}, u32[]{:S(2)}) collective-permute-start(bf16[136,768]{1,0:T(8,128)(2,1)S(1)} %back.1.refs_4_.refs_0_), channel_id=1, source_target_pairs={{0,8},{4,12},{8,0},{12,4},{1,9},{5,13},{9,1},{13,5},{2,10},{6,14},... | collective-permute-start | bytes 626696 | tf_op jit(solution)/shard_map/ppermute | solution.py:359
  62.7 13.8 %collective-permute-start.9 = (bf16[136,768]{1,0:T(8,128)(2,1)S(1)}, bf16[136,768]{1,0:T(8,128)(2,1)S(1)}, u32[]{:S(2)}, u32[]{:S(2)}) collective-permute-start(bf16[136,768]{1,0:T(8,128)(2,1)S(1)} %back.1.refs_4_.refs_0_), channel_id=1, source_target_pairs={{0,12},{4,8},{8,4},{12,0},{1,13},{5,9},{9,5},{13,1},{2,14},{6,10},... | collective-permute-start | bytes 626696 | tf_op jit(solution)/shard_map/ppermute | solution.py:359
  (9 other events, 7.9 us)
